TPU v7x, 32 devices: a whole 2x2x4 slice. The times are simulated.
32 devices in a mesh: wide: 16 (over z, x, core), grp: 2 (over y).
Axes of the slice: x: 2, y: 2, z: 4, core: 2. Of those that a mesh axis runs over, the one named last changes fastest.
Arguments:
- tokens: bfloat16 [2, 32, 196, 768], P(None, ('wide', 'grp')), may hold values from -6 to 6
- cotangent: bfloat16 [2, 32, 196, 768], P(None, ('wide', 'grp')), may hold values from -6 to 6
- window_place: int32 [2, 32], P(None, ('wide', 'grp')), may hold values from 0 to 25
- master: float32 [55424, 128], P('grp'), may hold values from -2 to 2
- first_moment: float32 [55424, 128], P('grp'), may hold values from -3 to 3
- second_moment: float32 [55424, 128], P('grp'), may hold values from 0.05 to 1
Outputs:
- block_out: bfloat16 [2, 32, 196, 768], P(None, ('wide', 'grp'))
- input_grad: bfloat16 [2, 32, 196, 768], P(None, ('wide', 'grp'))
- grads: float32 [55424, 128], P('grp')
- master_next: float32 [55424, 128], P('grp')
- moment_next: float32 [55424, 128], P('grp')
- second_next: float32 [55424, 128], P('grp')
- weights_next: bfloat16 [55424, 128], replicated
- proj_bias_grad: float32 [768], replicated
Inputs may be any that keep to these rules, and one draw needn't show every extreme that they name: `window_place`: place of a slot's window in its image's grid of 5 x 5 windows of 14 x 14 tokens, row by row, over the 64 x 64 token grid zero-padded at its ends; 25 marks an empty slot.
All inputs are finite; a program needn't handle non-finite values.
Results may differ from a plain program's by a relative error of at most 0.018.
Values may be sent and summed in bfloat16 or wider, within the bound.
No kernel may reach another device: no remote copies, remote signals or barrier semaphores. Data moves between devices by JAX's collectives and lax.ppermute only.
A program may use at most 320 MiB of HBM per device.

v0:
```python
import functools
import math

import jax
import jax.numpy as jnp
from jax import lax
from jax.experimental import pallas as pl
from jax.experimental.pallas import tpu as pltpu
from jax.sharding import PartitionSpec as P

FF = 3072
HD = 64
WS = 14
GRID = 64
ADAM_STEP = 10


EPS_NORM = 1e-06
BETA_ONE = 0.9
BETA_TWO = 0.95
ADAM_EPS = 1e-08
LEARN_RATE = 0.02
DECAY_RATE = 0.1


def layout(feature):
    rel_span = 2 * WS - 1
    return [
        (feature, 3 * feature),
        (2 * feature,),
        (feature, feature),
        (feature,),
        (feature, FF),
        (FF,),
        (FF, feature),
        (feature,),
        (feature,),
        (feature,),
        (feature,),
        (feature,),
        (rel_span, HD),
        (rel_span, HD),
    ]


CHUNK = 2304


def unpack_kernel(rows_ref, *refs, plan):
    *out_refs, raw_ref, wide_ref, sems = refs
    step = pl.program_id(0)
    limit = raw_ref.shape[1]
    total = sum(count for _, count, _ in plan)

    def chunk_copy(index, slot):
        start = jnp.int32(0)
        before = 0
        for row, count, _ in plan:
            at = row // 16 * 16 + (index - before) * CHUNK
            start = jnp.where(index >= before, at, start)
            before += count
        return pltpu.make_async_copy(
            rows_ref.at[pl.ds(pl.multiple_of(start, 16), limit), :], raw_ref.at[slot], sems.at[slot]
        )

    slot = lax.rem(step, 2)

    @pl.when(step == 0)
    def _():
        chunk_copy(step, slot).start()

    @pl.when(step + 1 < total)
    def _():
        chunk_copy(step + 1, 1 - slot).start()

    chunk_copy(step, slot).wait()
    part = limit // 5

    def widen(i, carry):
        at = pl.multiple_of(i * part, 16)
        wide_ref[pl.ds(at, part), :] = raw_ref[slot, pl.ds(at, part), :].astype(jnp.float32)
        return carry

    lax.fori_loop(0, 5, widen, 0)
    before = 0
    for (row, count, width), out_ref in zip(plan, out_refs):

        @pl.when((step >= before) & (step < before + count))
        def _(row=row, width=width, out_ref=out_ref):
            for j in range(width):
                picked = wide_ref[pl.ds(row % 16 + j, CHUNK // width, stride=width), :]
                out_ref[:, j * 128 : (j + 1) * 128] = picked.astype(jnp.bfloat16)

        before += count


def unpack_matrices(rows, dims, starts):
    plan = tuple(
        (start, math.prod(dims_of) // 128 // CHUNK, dims_of[1] // 128)
        for start, dims_of in zip(starts, dims)
    )
    specs = []
    before = 0
    for (_, count, width), dims_of in zip(plan, dims):

        def place(i, before=before, count=count):
            return (jnp.clip(i - before, 0, count - 1), 0)

        specs.append(pl.BlockSpec((CHUNK // width, dims_of[1]), place))
        before += count
    return pl.pallas_call(
        functools.partial(unpack_kernel, plan=plan),
        grid=(before,),
        in_specs=[pl.BlockSpec(memory_space=pl.ANY)],
        out_specs=specs,
        out_shape=[jax.ShapeDtypeStruct(dims_of, jnp.bfloat16) for dims_of in dims],
        scratch_shapes=[
            pltpu.VMEM((2, CHUNK + 16, 128), jnp.bfloat16),
            pltpu.VMEM((CHUNK + 16, 128), jnp.float32),
            pltpu.SemaphoreType.DMA((2,)),
        ],
        name="unpack_matrices",
    )(rows)


def unpack(rows, feature):
    dims = layout(feature)
    starts = []
    row = 0
    for dims_of in dims[:8]:
        starts.append(row)
        row = row + math.prod(dims_of) // 128
    matrices = unpack_matrices(rows, dims[:8:2], starts[:8:2])
    members = []
    for index, dims_of in enumerate(dims[:8]):
        if index % 2 == 0:
            members.append(matrices[index // 2])
        else:
            start = starts[index]
            members.append(rows[start : start + dims_of[0] // 128].reshape(dims_of))
    tail_size = sum(math.prod(dims_of) for dims_of in dims[8:])
    tail = rows[row : row - (-tail_size // 128)].reshape(-1)
    offset = 0
    for dims_of in dims[8:]:
        length = math.prod(dims_of)
        members.append(tail[offset : offset + length].reshape(dims_of))
        offset = offset + length
    return tuple(members)


def token_mask(window_place):
    cells = jnp.arange(WS * WS, dtype=jnp.int32)
    inner_row = cells // WS
    inner_col = cells % WS
    places = window_place[..., None]
    live_slot = places < 25
    row_real = WS * (places // 5) + inner_row < GRID
    col_real = WS * (places % 5) + inner_col < GRID
    return jnp.where(live_slot & row_real & col_real, 1.0, 0.0).astype(jnp.float32)


def normalize(inputs):
    row_mean = jnp.mean(inputs, -1, keepdims=True)
    centred = inputs - row_mean
    inv_scale = lax.rsqrt(jnp.mean(centred * centred, -1, keepdims=True) + EPS_NORM)
    return (centred * inv_scale, inv_scale)


def norm_back(grad_hat, normed_hat, inv_scale):
    first_mean = jnp.mean(grad_hat, -1, keepdims=True)
    second_mean = jnp.mean(grad_hat * normed_hat, -1, keepdims=True)
    return inv_scale * (grad_hat - first_mean - normed_hat * second_mean)


def attend_kernel(q_ref, k_ref, v_ref, table_ref, shift_ref, key_ref, probs_ref, out_ref):
    shift = shift_ref[...]
    key_cells = key_ref[...]
    row_count = shift.shape[0]
    real_key = lax.broadcasted_iota(jnp.int32, (row_count, row_count), 1) < WS * WS
    for part in range(2):
        cut = slice(part * HD, (part + 1) * HD)
        queries = q_ref[:, cut]
        along = jnp.dot(queries, table_ref[...], preferred_element_type=jnp.float32)
        for bit in (1, 2, 4, 8):
            along = jnp.where((shift & bit) != 0, pltpu.roll(along, 128 - bit, 1), along)
        high = along.astype(jnp.bfloat16)
        low = (along - high.astype(jnp.float32)).astype(jnp.bfloat16)
        scores = dot_last(queries, k_ref[:, cut]) * (1.0 / math.sqrt(HD))
        scores = scores + dot_last(high, key_cells) + dot_last(low, key_cells)
        scores = jnp.where(real_key, scores, -1e30)
        powers = jnp.exp(scores - jnp.max(scores, -1, keepdims=True))
        probs = (powers / jnp.sum(powers, -1, keepdims=True)).astype(jnp.bfloat16)
        probs_ref[0, part] = probs
        out_ref[:, cut] = jnp.dot(
            probs, v_ref[:, cut], preferred_element_type=jnp.float32
        ).astype(jnp.bfloat16)


def attend_back_kernel(
    q_ref, k_ref, v_ref, probs_ref, grad_ref, table_ref, shift_ref, key_ref,
    dq_ref, dk_ref, dv_ref, dtable_ref,
):
    shift = shift_ref[...]
    key_cells = key_ref[...]
    scale = 1.0 / math.sqrt(HD)

    @pl.when((pl.program_id(0) == 0) & (pl.program_id(1) == 0))
    def _():
        dtable_ref[...] = jnp.zeros(dtable_ref.shape, jnp.float32)

    for part in range(2):
        cut = slice(part * HD, (part + 1) * HD)
        queries = q_ref[:, cut]
        grad = grad_ref[:, cut]
        probs = probs_ref[0, part]
        dv_ref[:, cut] = dot_first(probs, grad).astype(jnp.bfloat16)
        grad_probs = dot_last(grad, v_ref[:, cut])
        wide_probs = probs.astype(jnp.float32)
        inner = jnp.sum(wide_probs * grad_probs, -1, keepdims=True)
        grad_scores = (wide_probs * (grad_probs - inner)).astype(jnp.bfloat16)
        dk_ref[:, cut] = (dot_first(grad_scores, queries) * scale).astype(jnp.bfloat16)
        along = jnp.dot(grad_scores, key_cells, preferred_element_type=jnp.float32)
        for bit in (1, 2, 4, 8):
            along = jnp.where((shift & bit) != 0, pltpu.roll(along, bit, 1), along)
        high = along.astype(jnp.bfloat16)
        low = (along - high.astype(jnp.float32)).astype(jnp.bfloat16)
        grad_query = jnp.dot(grad_scores, k_ref[:, cut], preferred_element_type=jnp.float32) * scale
        grad_query = grad_query + dot_last(high, table_ref[...]) + dot_last(low, table_ref[...])
        dq_ref[:, cut] = grad_query.astype(jnp.bfloat16)
        dtable_ref[...] += dot_first(queries, high) + dot_first(queries, low)


def window_constants(row_count):
    cells = jnp.arange(row_count, dtype=jnp.int32)[:, None]
    lanes = jnp.arange(128, dtype=jnp.int32)[None, :]
    first = lanes < 64
    shift = jnp.where(first, WS - 1 - cells // WS, WS - 1 - cells % WS)
    live = cells < WS * WS
    shift = jnp.where(live, shift, 0)
    offset = jnp.where(first, lanes, lanes - 64)
    place = jnp.where(first, cells // WS, cells % WS)
    key_cells = jnp.where(live & (offset == place), 1.0, 0.0).astype(jnp.bfloat16)
    return shift, key_cells


def wide_table(table_h, table_w):
    pad = jnp.zeros((HD, 64 - table_h.shape[0]), table_h.dtype)
    return jnp.concatenate([table_h[::-1].T, pad, table_w[::-1].T, pad], 1)


def attend(mixed, table, shift, key_cells, feature):
    rows, pairs = shift.shape[0], feature // 128
    wins = mixed.shape[0] // rows
    whole = lambda shape: pl.BlockSpec(shape, lambda w, h: (0,) * len(shape))
    column = lambda base: pl.BlockSpec((rows, 128), lambda w, h: (w, base * pairs + h))
    return pl.pallas_call(
        attend_kernel,
        grid=(wins, pairs),
        in_specs=[column(0), column(1), column(2), whole((HD, 128)), whole((rows, 128)), whole((rows, 128))],
        out_specs=[
            pl.BlockSpec((1, 2, rows, rows), lambda w, h: (w, h, 0, 0)),
            pl.BlockSpec((rows, 128), lambda w, h: (w, h)),
        ],
        out_shape=[
            jax.ShapeDtypeStruct((wins, 2 * pairs, rows, rows), jnp.bfloat16),
            jax.ShapeDtypeStruct((wins * rows, feature), jnp.bfloat16),
        ],
        name="attend",
    )(mixed, mixed, mixed, table, shift, key_cells)


def attend_back(mixed, probs, grad_att, table, shift, key_cells, feature):
    rows, pairs = shift.shape[0], feature // 128
    wins = mixed.shape[0] // rows
    whole = lambda shape: pl.BlockSpec(shape, lambda w, h: (0,) * len(shape))
    column = lambda base: pl.BlockSpec((rows, 128), lambda w, h: (w, base * pairs + h))
    flat = jax.ShapeDtypeStruct((wins * rows, feature), jnp.bfloat16)
    return pl.pallas_call(
        attend_back_kernel,
        grid=(wins, pairs),
        in_specs=[
            column(0), column(1), column(2),
            pl.BlockSpec((1, 2, rows, rows), lambda w, h: (w, h, 0, 0)),
            column(0),
            whole((HD, 128)), whole((rows, 128)), whole((rows, 128)),
        ],
        out_specs=[column(0), column(0), column(0), whole((HD, 128))],
        out_shape=[flat, flat, flat, jax.ShapeDtypeStruct((HD, 128), jnp.float32)],
        name="attend_back",
    )(mixed, mixed, mixed, probs, grad_att, table, shift, key_cells)


def dot_last(left, right):
    return lax.dot_general(left, right, (((1,), (1,)), ((), ())), preferred_element_type=jnp.float32)


def dot_first(left, right):
    return lax.dot_general(left, right, (((0,), (0,)), ((), ())), preferred_element_type=jnp.float32)


ORDERS = (("y", "x", "near"), ("x", "near", "y"), ("near", "y", "x"))


def halves(wide_size, group_size):
    return (wide_size, group_size) == (16, 2)


def pack_kernel(
    n1_ref, dq_ref, dk_ref, dv_ref, att_ref, dproj_ref, n2_ref, dpre_ref, act_ref, dout_ref, tail_ref,
    *refs, part_rows, share_rows, group_size, wide_size, cuts, relative,
):
    *out_refs, rows_ref, stage_ref, bias_ref, stage_sems = refs
    kept_refs, sent_refs = out_refs[: len(cuts)], out_refs[len(cuts) :]
    count = n1_ref.shape[0]
    ones = jnp.ones((16, count), jnp.bfloat16)

    def weight(base, left_ref, right_refs):
        width = sum(ref.shape[1] for ref in right_refs) // 128

        def block(f, carry):
            left = left_ref[:, pl.ds(pl.multiple_of(f * 128, 128), 128)]
            column = 0
            for ref in right_refs:
                product = dot_first(left, ref[...])
                for j in range(ref.shape[1] // 128):
                    rows_ref[pl.ds(base + f * 128 * width + column, 128, stride=width), :] = product[
                        :, j * 128 : (j + 1) * 128
                    ]
                    column += 1
            return carry

        lax.fori_loop(0, left_ref.shape[1] // 128, block, 0)
        return base + left_ref.shape[1] * width

    def bias(base, ref):
        total = jnp.dot(ones, ref[...], preferred_element_type=jnp.float32)
        for j in range(ref.shape[1] // 128):
            rows_ref[base + j : base + j + 1, :] = total[0:1, j * 128 : (j + 1) * 128]
        return base + ref.shape[1] // 128

    share = share_rows // wide_size
    own_wide = lax.axis_index("wide")
    own_group = lax.axis_index("grp")
    chunks = []
    for owner in range(group_size):
        for place in range(wide_size):
            low = place * share
            size = max(0, min(share, part_rows - low))
            chunks.append((owner, place, owner * part_rows + low, size))
    flying = {}
    sent = 0
    bias_known = False

    def pieces(slot, owner, place):
        if not relative:
            return [(stage_ref.at[slot], kept_refs[0].at[owner, place], None)]
        flips = place ^ own_wide
        flip = {
            "y": owner ^ own_group,
            "x": (flips >> 1) & 1,
            "near": (flips >> 2) & 1,
            "far": (flips >> 3) & 1,
        }
        found = []
        for (low, high), order, kept_ref, sent_ref in zip(cuts, ORDERS, kept_refs, sent_refs):
            spot = tuple(flip[name] for name in order + ("far",))
            source = stage_ref.at[slot, pl.ds(low, high - low), :]
            found.append((source, kept_ref.at[spot], sent_ref.at[spot]))
        return found

    def launch(slot, owner, place):
        for source, kept, other in pieces(slot, owner, place):

            def start(target, source=source):
                pltpu.make_async_copy(source, target, stage_sems.at[slot]).start()

            if other is None:
                start(kept)
            else:
                other_core = ((place ^ own_wide) & 1) == 1
                pl.when(other_core)(functools.partial(start, other))
                pl.when(jnp.logical_not(other_core))(functools.partial(start, kept))

    def finish(slot):
        if slot in flying:
            for source, kept, _ in pieces(slot, *flying.pop(slot)):
                pltpu.make_async_copy(source, kept, stage_sems.at[slot]).wait()

    def emit(upto):
        nonlocal sent
        while sent < len(chunks) and chunks[sent][2] + chunks[sent][3] <= upto:
            if chunks[sent][3] < share and not bias_known:
                break
            owner, place, source, size = chunks[sent]
            slot = sent % 2
            finish(slot)

            def convert(at, count, source=source, slot=slot):
                stage_ref[slot, pl.ds(at, count), :] = rows_ref[
                    pl.ds(pl.multiple_of(source + at, 16), count), :
                ].astype(jnp.bfloat16)

            def convert_block(i, carry, convert=convert):
                convert(pl.multiple_of(i * 128, 128), 128)
                return carry

            lax.fori_loop(0, size // 128, convert_block, 0)
            if size % 128:
                convert(size - size % 128, size % 128)
            if size < share:
                bias_place = part_rows - place * share
                first = max(0, -bias_place)
                stage_ref[slot, size:share, :] = bias_ref[first : first + share - size, :]
            launch(slot, owner, place)
            flying[slot] = (owner, place)
            sent += 1

    row = weight(0, n1_ref, [dq_ref, dk_ref, dv_ref])
    row = bias(row, dq_ref)
    row = bias(row, dv_ref)
    emit(row)
    row = weight(row, att_ref, [dproj_ref])
    proj_bias = row
    row = bias(row, dproj_ref)
    bias_size = dproj_ref.shape[1] // 128
    spare = share_rows - part_rows
    bias_ref[...] = jnp.concatenate(
        [
            rows_ref[proj_bias : proj_bias + bias_size, :],
            jnp.zeros((spare - bias_size, 128), jnp.float32),
        ],
        0,
    ).astype(jnp.bfloat16)
    bias_known = True
    emit(row)
    row = weight(row, n2_ref, [dpre_ref])
    row = bias(row, dpre_ref)
    emit(row)
    row = weight(row, act_ref, [dout_ref])
    row = bias(row, dout_ref)
    emit(row)
    rows_ref[row : row + tail_ref.shape[0], :] = tail_ref[...]
    emit(group_size * part_rows)
    for slot in range(2):
        finish(slot)


def pack_shares(factors, tail, part_rows, group_size, wide_size):
    feature = factors[0].shape[1]
    grain = 16 * wide_size
    share_rows = -(-(part_rows + feature // 128) // grain) * grain
    spare = share_rows - part_rows
    share = share_rows // wide_size
    relative = halves(wide_size, group_size)
    whole = pl.BlockSpec(memory_space=pltpu.VMEM)
    if relative:
        units = share // 16
        ends = [0, (units + 2) // 3 * 16, ((units + 2) // 3 + (units + 1) // 3) * 16, share]
        cuts = tuple(zip(ends, ends[1:]))
        shapes = [(2, 2, 2, 2, high - low, 128) for low, high in cuts] * 2
    else:
        cuts = ((0, share),)
        shapes = [(group_size, wide_size, share, 128)]
    return pl.pallas_call(
        functools.partial(
            pack_kernel,
            part_rows=part_rows,
            share_rows=share_rows,
            group_size=group_size,
            wide_size=wide_size,
            cuts=cuts,
            relative=relative,
        ),
        in_specs=[whole] * (len(factors) + 1),
        out_specs=[pl.BlockSpec(memory_space=pl.ANY)] * len(shapes),
        out_shape=[jax.ShapeDtypeStruct(shape, jnp.bfloat16) for shape in shapes],
        scratch_shapes=[
            pltpu.VMEM((group_size * part_rows, 128), jnp.float32),
            pltpu.VMEM((2, share, 128), jnp.bfloat16),
            pltpu.VMEM((spare, 128), jnp.bfloat16),
            pltpu.SemaphoreType.DMA((2,)),
        ],
        compiler_params=pltpu.CompilerParams(vmem_limit_bytes=60 * 1024 * 1024),
        name="pack_grads",
    )(*factors, tail)


def gelu_slope(pre_act):
    normal_cdf = 0.5 * (1.0 + jax.scipy.special.erf(pre_act / math.sqrt(2.0)))
    return normal_cdf + pre_act * jnp.exp(-0.5 * pre_act * pre_act) / math.sqrt(2.0 * math.pi)


def window_pass(tokens, cotangent, keep_mask, weights):
    (
        qkv_w,
        qv_b,
        proj_w,
        proj_b,
        fc1_w,
        fc1_b,
        fc2_w,
        fc2_b,
        ln1_g,
        ln1_b,
        ln2_g,
        ln2_b,
        table_h,
        table_w,
    ) = weights
    win_count, tok_count, feature = tokens.shape
    row_count = win_count * tok_count
    inputs = tokens.reshape(row_count, feature).astype(jnp.float32)
    keep_rows = keep_mask.reshape(row_count, 1)
    hat_one, scale_one = normalize(inputs)
    normed_one = (
        (hat_one * ln1_g.astype(jnp.float32) + ln1_b.astype(jnp.float32)) * keep_rows
    ).astype(jnp.bfloat16)
    bias_full = jnp.concatenate(
        [qv_b[:feature], jnp.zeros((feature,), jnp.bfloat16), qv_b[feature:]]
    ).astype(jnp.float32)
    mixed = (jnp.dot(normed_one, qkv_w, preferred_element_type=jnp.float32) + bias_full).astype(
        jnp.bfloat16
    )
    shift, key_cells = window_constants(tok_count)
    table = wide_table(table_h, table_w)
    probs, attended = attend(mixed, table, shift, key_cells, feature)
    resid = keep_rows * (
        inputs
        + jnp.dot(attended, proj_w, preferred_element_type=jnp.float32)
        + proj_b.astype(jnp.float32)
    )
    hat_two, scale_two = normalize(resid)
    normed_two = (hat_two * ln2_g.astype(jnp.float32) + ln2_b.astype(jnp.float32)).astype(
        jnp.bfloat16
    )
    pre_act = jnp.dot(normed_two, fc1_w, preferred_element_type=jnp.float32) + fc1_b.astype(
        jnp.float32
    )
    activation = jax.nn.gelu(pre_act, approximate=False).astype(jnp.bfloat16)
    result = keep_rows * (
        resid
        + jnp.dot(activation, fc2_w, preferred_element_type=jnp.float32)
        + fc2_b.astype(jnp.float32)
    )
    cot_rows = cotangent.reshape(row_count, feature).astype(jnp.float32) * keep_rows
    grad_out = cot_rows.astype(jnp.bfloat16)
    grad_act = jnp.einsum("nd,fd->nf", grad_out, fc2_w, preferred_element_type=jnp.float32)
    grad_pre = (grad_act * gelu_slope(pre_act)).astype(jnp.bfloat16)
    grad_norm_two = jnp.einsum("nf,df->nd", grad_pre, fc1_w, preferred_element_type=jnp.float32)
    grad_ln2_g = jnp.sum(grad_norm_two * hat_two, 0)
    grad_ln2_b = jnp.sum(grad_norm_two, 0)
    grad_resid = cot_rows + norm_back(grad_norm_two * ln2_g.astype(jnp.float32), hat_two, scale_two)
    grad_branch = keep_rows * grad_resid
    grad_proj = grad_branch.astype(jnp.bfloat16)
    grad_att = jnp.einsum(
        "ne,de->nd", grad_proj, proj_w, preferred_element_type=jnp.float32
    ).astype(jnp.bfloat16)
    grad_query, grad_keys, grad_values, grad_table = attend_back(
        mixed, probs, grad_att, table, shift, key_cells, feature
    )
    rel_span = table_h.shape[0]
    grad_table_h = grad_table[:, :rel_span].T[::-1]
    grad_table_w = grad_table[:, 64 : 64 + rel_span].T[::-1]
    grad_mixed = jnp.concatenate([grad_query, grad_keys, grad_values], -1)
    grad_norm_one = keep_rows * jnp.einsum(
        "nf,df->nd", grad_mixed, qkv_w, preferred_element_type=jnp.float32
    )
    grad_ln1_g = jnp.sum(grad_norm_one * hat_one, 0)
    grad_ln1_b = jnp.sum(grad_norm_one, 0)
    grad_input = grad_branch + norm_back(
        grad_norm_one * ln1_g.astype(jnp.float32), hat_one, scale_one
    )
    factors = (
        normed_one,
        grad_query,
        grad_keys,
        grad_values,
        attended,
        grad_proj,
        normed_two,
        grad_pre,
        activation,
        grad_out,
    )
    tail = (grad_ln1_g, grad_ln1_b, grad_ln2_g, grad_ln2_b, grad_table_h, grad_table_w)
    block_part = result.reshape(win_count, tok_count, feature).astype(jnp.bfloat16)
    input_part = grad_input.reshape(win_count, tok_count, feature).astype(jnp.bfloat16)
    return (block_part, input_part, factors, tail)


def swap(values, axis, bit):
    return lax.ppermute(values, axis, [(i, i ^ bit) for i in range(lax.axis_size(axis))])


def wide_bits(count):
    place = lax.axis_index("wide")
    return [(place >> bit) & 1 for bit in range(count)]


def splits(part_rows):
    return lax.axis_size("grp") == 2 and lax.axis_size("wide") % 8 == 0 and part_rows % 64 == 0


def eighth_index(core, cross, deep):
    return (core * 2 + cross) * 2 + deep


def gather_groups(mine, diagonal, finish):
    core, cross, deep = wide_bits(3)
    first = swap(mine, "grp", 1)
    diagonal, first = lax.optimization_barrier((diagonal, first))
    last = swap(diagonal, "grp", 1)
    side = swap(first, "wide", 2)
    back = swap(first, "wide", 4)
    near = (first, side, back, last)
    far = [swap(part, "wide", 1) for part in near]
    group = lax.axis_index("grp")
    out = finish(first)
    rows = out.shape[0] * out.shape[1]
    out = out.reshape((2, 8) + mine.shape)
    for parts, which in ((near, core), (far, 1 - core)):
        for part, flip_cross, flip_deep in zip(parts, (0, 1, 0, 1), (0, 0, 1, 1)):
            at = eighth_index(which, cross ^ flip_cross, deep ^ flip_deep)
            out = lax.dynamic_update_slice(out, part[None, None], (1 - group, at, 0, 0))
    return out.reshape(rows, 128)


def joined(kept, sent):
    return (kept.astype(jnp.float32) + sent.astype(jnp.float32)).astype(kept.dtype)


def reduce_shares(packed):
    if len(packed) == 1:
        rows = packed[0].reshape(-1, 128)
        return lax.psum_scatter(rows, ("grp", "wide"), scatter_dimension=0, tiled=True)
    moves = {
        "x": lambda v: swap(v, "wide", 2),
        "near": lambda v: swap(v, "wide", 4),
        "far": lambda v: swap(v, "wide", 8),
        "y": lambda v: swap(v, "grp", 1),
    }
    done = []
    for kept, sent, order in zip(packed[:3], packed[3:], ORDERS):
        arrived = swap(sent, "wide", 1)
        for name in order + ("far",):
            leaving = joined(kept[1], arrived[1])
            kept = joined(kept[0], arrived[0])
            arrived = moves[name](leaving)
        done.append(joined(kept, arrived))
    return jnp.concatenate(done, 0)


def own_eighths(rows):
    core, cross, deep = wide_bits(3)
    parts = rows.reshape(8, -1, 128)
    spots = (eighth_index(core, cross, deep), eighth_index(core, 1 - cross, 1 - deep))
    return [lax.dynamic_index_in_dim(parts, spot, keepdims=False) for spot in spots]


def first_step(grads, first_moment):
    return BETA_ONE * first_moment + (1.0 - BETA_ONE) * grads


def second_step(grads, master, moment_next, second_moment):
    second_next = BETA_TWO * second_moment + (1.0 - BETA_TWO) * grads * grads
    fix_one = 1.0 - BETA_ONE**ADAM_STEP
    fix_two = 1.0 - BETA_TWO**ADAM_STEP
    update = (
        moment_next / fix_one / (jnp.sqrt(second_next / fix_two) + ADAM_EPS) + DECAY_RATE * master
    )
    return (master - LEARN_RATE * update, second_next)


BLOCK_ROWS = 2048


def place_kernel(group_ref, master_ref, out_ref):
    out_ref[0] = master_ref[...].astype(jnp.bfloat16)


def place_own(master):
    rows = master.shape[0]
    return pl.pallas_call(
        place_kernel,
        grid_spec=pltpu.PrefetchScalarGridSpec(
            num_scalar_prefetch=1,
            grid=(pl.cdiv(rows, BLOCK_ROWS),),
            in_specs=[pl.BlockSpec((BLOCK_ROWS, 128), lambda i, g: (i, 0))],
            out_specs=pl.BlockSpec((1, BLOCK_ROWS, 128), lambda i, g: (g[0], i, 0)),
        ),
        out_shape=jax.ShapeDtypeStruct((2, rows, 128), jnp.bfloat16),
        name="place_own",
    )(lax.axis_index("grp").reshape(1), master)


def eighth_kernel(spot_ref, total_ref, master_ref, first_ref, second_ref, out_ref, *, factor):
    grads = total_ref[...].astype(jnp.float32) * factor
    moment = first_step(grads, first_ref[...])
    out_ref[0] = second_step(grads, master_ref[...], moment, second_ref[...])[0].astype(jnp.bfloat16)


def eighth_weights(totals, state, factor):
    size = state[0].shape[0] // 8
    core, cross, deep = wide_bits(3)
    spots = (eighth_index(core, cross, deep), eighth_index(core, 1 - cross, 1 - deep))
    both = pl.pallas_call(
        functools.partial(eighth_kernel, factor=factor),
        grid_spec=pltpu.PrefetchScalarGridSpec(
            num_scalar_prefetch=1,
            grid=(2,),
            in_specs=[pl.BlockSpec((size, 128), lambda i, spot: (spot[i], 0))] * 4,
            out_specs=pl.BlockSpec((1, size, 128), lambda i, spot: (i, 0, 0)),
        ),
        out_shape=jax.ShapeDtypeStruct((2, size, 128), jnp.bfloat16),
        name="eighth_weights",
    )(jnp.stack(spots).astype(jnp.int32), totals, *state)
    return both[0], both[1]


def adam_kernel(group_ref, total_ref, master_ref, first_ref, second_ref, *refs, factor):
    grads_ref, master_out, first_out, second_out, weights_ref = refs[-5:]
    grads = total_ref[...].astype(jnp.float32) * factor
    moment = first_step(grads, first_ref[...])
    master_next, second_next = second_step(grads, master_ref[...], moment, second_ref[...])
    grads_ref[...] = grads
    master_out[...] = master_next
    first_out[...] = moment
    second_out[...] = second_next
    weights_ref[0] = master_next.astype(jnp.bfloat16)


def adam_rows(totals, state, factor, first_block, last_block, onto, after):
    rows = state[0].shape[0]
    row_spec = pl.BlockSpec((BLOCK_ROWS, 128), lambda i, g: (first_block + i, 0))
    anywhere = pl.BlockSpec(memory_space=pl.ANY)
    wide = jax.ShapeDtypeStruct((rows, 128), jnp.float32)
    spare = 5 - len(onto)
    return pl.pallas_call(
        functools.partial(adam_kernel, factor=factor),
        grid_spec=pltpu.PrefetchScalarGridSpec(
            num_scalar_prefetch=1,
            grid=(last_block - first_block,),
            in_specs=[row_spec] * 4 + [anywhere] * (len(onto) + len(after)),
            out_specs=[row_spec] * 4
            + [pl.BlockSpec((1, BLOCK_ROWS, 128), lambda i, g: (g[0], first_block + i, 0))],
        ),
        out_shape=[wide] * 4 + [jax.ShapeDtypeStruct((2, rows, 128), jnp.bfloat16)],
        input_output_aliases={5 + i: spare + i for i in range(len(onto))},
        name="adam_rows",
    )(lax.axis_index("grp").reshape(1), totals, *state, *onto, *after)


def body(tokens, cotangent, window_place, master, first_moment, second_moment):
    part_rows = master.shape[0]
    wide_size = lax.axis_size("wide")
    group_size = lax.axis_size("grp")
    feature = tokens.shape[-1]
    micro_count, slots, tok_count, _ = tokens.shape
    masks = token_mask(window_place)
    if splits(part_rows):
        mine, diagonal = (part.astype(jnp.bfloat16) for part in own_eighths(master))
        gathered = gather_groups(mine, diagonal, lambda first: place_own(master))
    else:
        gathered = lax.all_gather(master.astype(jnp.bfloat16), "grp", axis=0, tiled=True)
    weights = unpack(gathered, feature)
    wins = micro_count * slots
    extra = -tok_count % 16

    def padded(values):
        values = values.reshape((wins,) + values.shape[2:])
        return jnp.pad(values, ((0, 0), (0, extra)) + ((0, 0),) * (values.ndim - 2))

    block_part, input_part, factors, tail = window_pass(
        padded(tokens), padded(cotangent), padded(masks), weights
    )
    filled = sum(math.prod(dims_of) for dims_of in layout(feature)[:8]) // 128
    tail = jnp.concatenate([member.reshape(-1) for member in tail])
    tail_rows = part_rows * group_size - filled
    tail = jnp.pad(tail, (0, tail_rows * 128 - tail.shape[0])).reshape(tail_rows, 128)
    packed = pack_shares(factors, tail, part_rows, group_size, wide_size)
    owned = reduce_shares(packed)
    block_out = block_part[:, :tok_count].reshape(tokens.shape)
    input_grad = input_part[:, :tok_count].reshape(tokens.shape)
    owned, block_out, input_grad = lax.optimization_barrier((owned, block_out, input_grad))
    totals = lax.all_gather(owned, "wide", axis=0, tiled=True)
    factor = 1.0 / (micro_count * wide_size * group_size)
    bias_total = totals[part_rows : part_rows + feature // 128]
    proj_bias_grad = bias_total.astype(jnp.float32).reshape(-1) * factor
    state = (master, first_moment, second_moment)
    if splits(part_rows):
        updated = []

        def finish(first):
            blocks = pl.cdiv(part_rows, BLOCK_ROWS)
            half = blocks // 2
            held = gathered.reshape(2, part_rows, 128)
            begun = adam_rows(totals, state, factor, 0, half, (held,), ())
            updated.extend(adam_rows(totals, state, factor, half, blocks, begun, (first,)))
            return updated.pop()

        mine, diagonal = eighth_weights(totals, state, factor)
        weights_next = gather_groups(mine, diagonal, finish)
        grads, master_next, moment_next, second_next = updated
    else:
        grads = totals[:part_rows].astype(jnp.float32) * factor
        moment_next = first_step(grads, first_moment)
        master_next, second_next = second_step(grads, master, moment_next, second_moment)
        own_weights = master_next.astype(jnp.bfloat16)
        weights_next = lax.all_gather(own_weights, "grp", axis=0, tiled=True)
    return (
        block_out,
        input_grad,
        grads,
        master_next,
        moment_next,
        second_next,
        weights_next,
        proj_bias_grad,
    )


def solution(mesh):
    return jax.shard_map(
        body,
        mesh=mesh,
        in_specs=(
            P(None, ("wide", "grp"), None, None),
            P(None, ("wide", "grp"), None, None),
            P(None, ("wide", "grp")),
            P("grp", None),
            P("grp", None),
            P("grp", None),
        ),
        out_specs=(
            P(None, ("wide", "grp"), None, None),
            P(None, ("wide", "grp"), None, None),
            P("grp", None),
            P("grp", None),
            P("grp", None),
            P("grp", None),
            P(),
            P(),
        ),
        check_vma=False,
    )
```

profile of v0, /device:TPU:0, one launch (start us, length us, event | category | flops | bytes accessed | tf_op | source)
XLA Modules:
  0.0 447.3 jit_solution(6138369844530413063)
XLA Ops:
  7.3 3.5 fusion.45
  10.8 3.0 collective-permute-start
  14.6 1.2 multiply_reduce_fusion.5
  16.6 13.2 %place_own.1 = bf16[2,27712,128]{2,1,0:T(8,128)(2,1)} custom-call(s32[1]{0:T(128)} %bitcast.2.group_ref, f32[27712,128]{1,0:T(8,128)} %master_ref.7), custom_call_target="tpu_custom_call" | custom-call | tf_op jit(solution)/shard_map/place_own/pallas_call | solution.py:683
  32.6 1.1 collective-permute-done
  33.8 1.7 collective-permute-start.1
  35.5 1.6 collective-permute-start.2
  37.0 1.5 collective-permute-start.3
  38.6 2.1 bitcast_dynamic-update-slice_fusion.15
  40.7 14.1 %collective-permute-done.1 = bf16[3464,128]{1,0:T(8,128)(2,1)S(1)} collective-permute-done((bf16[3464,128]{1,0:T(8,128)(2,1)}, bf16[3464,128]{1,0:T(8,128)(2,1)S(1)}, u32[]{:S(2)}, u32[]{:S(2)}) %collective-permute-start.1) | collective-permute-done | bytes 886816 | tf_op jit(solution)/shard_map/ppermute | solution.py:592
  54.8 1.2 collective-permute-done.2
  56.0 3.4 collective-permute-done.3
  59.4 1.0 bitcast_dynamic-update-slice_fusion.14
  62.3 1.0 bitcast_dynamic-update-slice_fusion.11
  63.3 1.0 bitcast_dynamic-update-slice_fusion.10
  64.2 1.0 bitcast_dynamic-update-slice_fusion.9
  65.2 1.0 bitcast_dynamic-update-slice_fusion.8
  67.0 21.1 %unpack_matrices.1 = (bf16[768,2304]{1,0:T(8,128)(2,1)}, bf16[768,768]{1,0:T(8,128)(2,1)}, bf16[768,3072]{1,0:T(8,128)(2,1)}, bf16[3072,768]{1,0:T(8,128)(2,1)}) custom-call(bf16[55424,128]{1,0:T(8,128)(2,1)} %bitcast.284), custom_call_target="tpu_custom_call" | custom-call | tf_op jit(solution)/shard_map/unpack_matrices/pallas_call | solution.py:111
  90.0 1.8 multiply_convert_fusion
  92.7 2.9 fusion.16.q_ref.k_ref.v_ref
  96.4 25.3 %attend.1 = (bf16[2,12,208,208]{3,2,1,0:T(8,128)(2,1)}, bf16[416,768]{1,0:T(8,128)(2,1)}) custom-call(bf16[416,2304]{1,0:T(8,128)(2,1)} %fusion.16.q_ref.k_ref.v_ref, bf16[416,2304]{1,0:T(8,128)(2,1)} %fusion.16.q_ref.k_ref.v_ref, bf16[416,2304]{1,0:T(8,128)(2,1)} %fusion.16.q_ref.k_ref.v_ref, bf16[64,128]{1,0:T(8,128)(2,1)} %pad_maximum_fusion.1.table_ref, ...), custom_call_target="tpu_custom_call" | custom-call | tf_op jit(solution)/shard_map/attend/pallas_call | solution.py:256
  121.7 2.3 fusion.93
  124.6 15.1 %fusion.8 = (bf16[416,3072]{1,0:T(8,128)(2,1)}, f32[416,3072]{1,0:T(8,128)S(1)}) fusion(f32[3072]{0:T(1024)S(1)} %fusion.74, bf16[416,768]{1,0:T(8,128)(2,1)S(1)} %add_convert_fusion.7.n2_ref, bf16[768,3072]{1,0:T(8,128)(2,1)} %get-tuple-element.48), kind=kOutput, calls=%fused_computation.10 | convolution fusion | flops 2047279104 | bytes 13037568 | tf_op jit(solution)/shard_map/dot_general | solution.py:536
  139.8 3.8 fusion.5.dpre_ref
  143.6 2.6 multiply_reduce_fusion.1
  146.2 1.7 fusion.89
  147.9 1.5 convolution_convert_fusion.grad_ref
  149.5 24.6 %attend_back.1 = (bf16[416,768]{1,0:T(8,128)(2,1)}, bf16[416,768]{1,0:T(8,128)(2,1)}, bf16[416,768]{1,0:T(8,128)(2,1)}, f32[64,128]{1,0:T(8,128)}) custom-call(bf16[416,2304]{1,0:T(8,128)(2,1)} %fusion.16.q_ref.k_ref.v_ref, bf16[416,2304]{1,0:T(8,128)(2,1)} %fusion.16.q_ref.k_ref.v_ref, bf16[416,2304]{1,0:T(8,128)(2,1)} %fusion.16.q_ref.k_ref.v_ref, ...), custom_call_target="tpu_custom_call" | custom-call | tf_op jit(solution)/shard_map/attend_back/pallas_call | solution.py:278
  175.5 5.5 %multiply_reduce_fusion = (f32[416]{0:T(512)S(1)}, f32[768]{0:T(1024)S(1)}, f32[416]{0:T(512)S(1)}, f32[768]{0:T(1024)S(1)}, f32[416,768]{1,0:T(8,128)}) fusion(f32[416,768]{1,0:T(8,128)S(1)} %copy-done.1, f32[768]{0:T(1024)S(1)} %get-tuple-element.93, bf16[768,2304]{1,0:T(8,128)(2,1)} %get-tuple-element.43, bf16[416,768]{1,0:T(8,128)(2,1)} %get-tuple-element.51.dv_ref, ...), kind=kOutput, calls=%fused_computation.58 | convolution fusion | flops 1480505088 | bytes 8025984 | tf_op jit(solution)/shard_map/nf,df->nd/dot_general | solution.py:565
  181.7 34.7 %pack_grads.1 = (bf16[2,2,2,2,592,128]{5,4,3,2,1,0:T(8,128)(2,1)}, bf16[2,2,2,2,576,128]{5,4,3,2,1,0:T(8,128)(2,1)}, bf16[2,2,2,2,576,128]{5,4,3,2,1,0:T(8,128)(...) custom-call(bf16[416,768]{1,0:T(8,128)(2,1)} %copy-done.4, ...), custom_call_target="tpu_custom_call" | custom-call | tf_op jit(solution)/shard_map/pack_grads/pallas_call | solution.py:464
  217.5 3.9 collective-permute-done.18
  221.4 2.4 add_convert_fusion.3
  226.0 2.3 collective-permute-done.8
  228.9 1.6 collective-permute-start.9
  230.5 2.1 fusion.30
  232.6 19.5 %collective-permute-done.19 = bf16[2,2,2,576,128]{4,3,2,1,0:T(8,128)(2,1)S(1)} collective-permute-done((bf16[2,2,2,576,128]{4,3,2,1,0:T(8,128)(2,1)S(1)}, bf16[2,2,2,576,128]{4,3,2,1,0:T(8,128)(2,1)S(1)}, u32[]{:S(2)}, u32[]{:S(2)}) %collective-permute-start.19) | collective-permute-done | bytes 1179680 | tf_op jit(solution)/shard_map/ppermute | solution.py:592
  252.4 1.6 collective-permute-start.20
  255.0 3.5 collective-permute-done.9
  259.8 1.3 copy.65
  261.1 1.3 copy.64
  262.4 8.1 %collective-permute-done.20 = bf16[2,2,576,128]{3,2,1,0:T(8,128)(2,1)S(1)} collective-permute-done((bf16[2,2,576,128]{3,2,1,0:T(8,128)(2,1)S(1)}, bf16[2,2,576,128]{3,2,1,0:T(8,128)(2,1)S(1)}, u32[]{:S(2)}, u32[]{:S(2)}) %collective-permute-start.20) | collective-permute-done | bytes 589856 | tf_op jit(solution)/shard_map/ppermute | solution.py:592
  271.4 1.6 collective-permute-start.16
  274.5 5.2 %collective-permute-done.21 = bf16[2,576,128]{2,1,0:T(8,128)(2,1)S(1)} collective-permute-done((bf16[2,576,128]{2,1,0:T(8,128)(2,1)S(1)}, bf16[2,576,128]{2,1,0:T(8,128)(2,1)S(1)}, u32[]{:S(2)}, u32[]{:S(2)}) %collective-permute-start.21) | collective-permute-done | bytes 294944 | tf_op jit(solution)/shard_map/ppermute | solution.py:592
  279.8 2.6 collective-permute-start.22
  282.9 2.6 collective-permute-start.12
  285.5 10.5 %collective-permute-done.22 = bf16[576,128]{1,0:T(8,128)(2,1)S(1)} collective-permute-done((bf16[576,128]{1,0:T(8,128)(2,1)S(1)}, bf16[576,128]{1,0:T(8,128)(2,1)S(1)}, u32[]{:S(2)}, u32[]{:S(2)}) %collective-permute-start.22) | collective-permute-done | bytes 147488 | tf_op jit(solution)/shard_map/ppermute | solution.py:592
  296.1 3.1 collective-permute-done.17
  299.3 2.3 collective-permute-done.12
  303.0 65.2 %all-gather.2.cloned.1.call-done.total_ref = bf16[27904,128]{1,0:T(8,128)(2,1)} async-done(((bf16[1744,128]{1,0:T(8,128)(2,1)}), bf16[27904,128]{1,0:T(8,128)(2,1)}) %all-gather.2.cloned.1.call-update) | async-done | bytes 7143440 | tf_op jit(solution)/shard_map/all_gather | solution.py:785
  368.3 7.7 %eighth_weights.1 = bf16[2,3464,128]{2,1,0:T(8,128)(2,1)} custom-call(s32[2]{0:T(128)} %pad_add_fusion.spot_ref, bf16[27904,128]{1,0:T(8,128)(2,1)} %all-gather.2.cloned.1.call-done.total_ref, f32[27712,128]{1,0:T(8,128)} %master_ref.7, f32[27712,128]{1,0:T(8,128)} %first_ref.5, f32[27712,128]{1,0:T(8,128)} %second_ref.5), custom_call_target="tpu_custom_call" | custom-call | tf_op jit(solution)/shard_map/eighth_weights/pallas_call | solution.py:706
  376.0 1.5 slice_bitcast_fusion
  377.5 1.5 collective-permute-start.23
  379.1 23.8 %adam_rows.2 = (f32[27712,128]{1,0:T(8,128)}, f32[27712,128]{1,0:T(8,128)}, f32[27712,128]{1,0:T(8,128)}, f32[27712,128]{1,0:T(8,128)}, bf16[2,27712,128]{2,1,0:T(8,128)(2,1)}) custom-call(s32[1]{0:T(128)} %bitcast.2.group_ref, bf16[27904,128]{1,0:T(8,128)(2,1)} %all-gather.2.cloned.1.call-done.total_ref, ...), custom_call_target="tpu_custom_call", output_to_operand_aliasing={{4}: (5, {})} | custom-call | tf_op jit(solution)/shard_map/adam_rows/pallas_call | solution.py:738
  402.8 1.3 multiply_bitcast_fusion
  404.7 1.5 collective-permute-start.25
  406.8 21.4 %adam_rows.3 = (f32[27712,128]{1,0:T(8,128)}, f32[27712,128]{1,0:T(8,128)}, f32[27712,128]{1,0:T(8,128)}, f32[27712,128]{1,0:T(8,128)}, bf16[2,27712,128]{2,1,0:T(8,128)(2,1)}) custom-call(s32[1]{0:T(128)} %bitcast.2.group_ref, ...), custom_call_target="tpu_custom_call", output_to_operand_aliasing={{0}: (5, {}), {1}: (6, {}), {2}: (7, {}), {3}: (8, {}), {4}... | custom-call | tf_op jit(solution)/shard_map/adam_rows/pallas_call | solution.py:738
  428.2 2.1 bitcast_dynamic-update-slice_fusion.7
  430.6 2.1 bitcast_dynamic-update-slice_fusion.6
  433.0 1.0 bitcast_dynamic-update-slice_fusion.5
  434.2 1.0 bitcast_dynamic-update-slice_fusion.4
  435.1 2.1 bitcast_dynamic-update-slice_fusion.3
  437.3 1.0 bitcast_dynamic-update-slice_fusion.2
  438.3 1.0 bitcast_dynamic-update-slice_fusion.1
  439.2 1.0 bitcast_dynamic-update-slice_fusion
  (164 shorter events, 26.3 us)
Async XLA Ops:
  7.2 6.6 %copy-start.16 = (s32[2,1]{0,1:T(1,128)S(1)}, s32[2,1]{0,1:T(1,128)}, u32[]{:S(2)}) copy-start(s32[2,1]{0,1:T(1,128)} %param.8) | copy-start | bytes 28
  7.2 6.7 %copy-start = (bf16[2,1,196,768]{3,0,2,1:T(2,128)(2,1)S(1)}, bf16[2,1,196,768]{3,0,2,1:T(2,128)(2,1)}, u32[]{:S(2)}) copy-start(bf16[2,1,196,768]{3,0,2,1:T(2,128)(2,1)} %param.6) | copy-start | bytes 1806340
  7.2 361.1 %all-gather.2.cloned.1.call-start = ((), (), s32[]{:S(2)}) async-start(), calls=%async_computation | async-start | bytes 7589888 | tf_op jit(solution)/shard_map/all_gather | solution.py:785
  10.8 23.0 %collective-permute-start = (bf16[3464,128]{1,0:T(8,128)(2,1)}, bf16[3464,128]{1,0:T(8,128)(2,1)}, u32[]{:S(2)}, u32[]{:S(2)}) collective-permute-start(bf16[3464,128]{1,0:T(8,128)(2,1)} %get-tuple-element.94), channel_id=1, source_target_pairs={{0,1},{1,0},{2,3},{3,2},{4,5},{5,4},{6,7},{7,6},{8,9},{9,8},{10,11... | collective-permute-start | bytes 2660360 | tf_op jit(solution)/shard_map/ppermute | solution.py:592
  29.8 1.1 copy-start.14
  33.8 21.1 %collective-permute-start.1 = (bf16[3464,128]{1,0:T(8,128)(2,1)}, bf16[3464,128]{1,0:T(8,128)(2,1)S(1)}, u32[]{:S(2)}, u32[]{:S(2)}) collective-permute-start(bf16[3464,128]{1,0:T(8,128)(2,1)} %collective-permute-done), channel_id=1, source_target_pairs={{0,4},{2,6},{4,0},{6,2},{8,12},{10,14},{12,8},{14,10},{16,20},{18,... | collective-permute-start | bytes 2660360 | tf_op jit(solution)/shard_map/ppermute | solution.py:592
  35.5 20.5 %collective-permute-start.2 = (bf16[3464,128]{1,0:T(8,128)(2,1)}, bf16[3464,128]{1,0:T(8,128)(2,1)S(1)}, u32[]{:S(2)}, u32[]{:S(2)}) collective-permute-start(bf16[3464,128]{1,0:T(8,128)(2,1)} %collective-permute-done), channel_id=1, source_target_pairs={{0,8},{2,10},{4,12},{6,14},{8,0},{10,2},{12,4},{14,6},{16,24},{18,... | collective-permute-start | bytes 2660360 | tf_op jit(solution)/shard_map/ppermute | solution.py:592
  37.0 25.2 %collective-permute-start.4 = (bf16[3464,128]{1,0:T(8,128)(2,1)}, bf16[3464,128]{1,0:T(8,128)(2,1)S(1)}, u32[]{:S(2)}, u32[]{:S(2)}) collective-permute-start(bf16[3464,128]{1,0:T(8,128)(2,1)} %collective-permute-done), channel_id=1, source_target_pairs={{0,2},{2,0},{4,6},{6,4},{8,10},{10,8},{12,14},{14,12},{16,18},{18,... | collective-permute-start | bytes 2660360 | tf_op jit(solution)/shard_map/ppermute | solution.py:592
  37.0 22.3 %collective-permute-start.3 = (bf16[3464,128]{1,0:T(8,128)(2,1)}, bf16[3464,128]{1,0:T(8,128)(2,1)S(1)}, u32[]{:S(2)}, u32[]{:S(2)}) collective-permute-start(bf16[3464,128]{1,0:T(8,128)(2,1)} %get-tuple-element.42), channel_id=1, source_target_pairs={{0,1},{1,0},{2,3},{3,2},{4,5},{5,4},{6,7},{7,6},{8,9},{9,8},{10,11... | collective-permute-start | bytes 2660360 | tf_op jit(solution)/shard_map/ppermute | solution.py:592
  54.8 8.4 %collective-permute-start.5 = (bf16[3464,128]{1,0:T(8,128)(2,1)S(1)}, bf16[3464,128]{1,0:T(8,128)(2,1)S(1)}, u32[]{:S(2)}, u32[]{:S(2)}) collective-permute-start(bf16[3464,128]{1,0:T(8,128)(2,1)S(1)} %collective-permute-done.1), channel_id=1, source_target_pairs={{0,2},{2,0},{4,6},{6,4},{8,10},{10,8},{12,14},{14,12},{16,18},{18,... | collective-permute-start | bytes 2660360 | tf_op jit(solution)/shard_map/ppermute | solution.py:592
  56.0 8.3 %collective-permute-start.6 = (bf16[3464,128]{1,0:T(8,128)(2,1)S(1)}, bf16[3464,128]{1,0:T(8,128)(2,1)S(1)}, u32[]{:S(2)}, u32[]{:S(2)}) collective-permute-start(bf16[3464,128]{1,0:T(8,128)(2,1)S(1)} %collective-permute-done.2), channel_id=1, source_target_pairs={{0,2},{2,0},{4,6},{6,4},{8,10},{10,8},{12,14},{14,12},{16,18},{18,... | collective-permute-start | bytes 2660360 | tf_op jit(solution)/shard_map/ppermute | solution.py:592
  59.4 5.8 %collective-permute-start.7 = (bf16[3464,128]{1,0:T(8,128)(2,1)S(1)}, bf16[3464,128]{1,0:T(8,128)(2,1)S(1)}, u32[]{:S(2)}, u32[]{:S(2)}) collective-permute-start(bf16[3464,128]{1,0:T(8,128)(2,1)S(1)} %collective-permute-done.3), channel_id=1, source_target_pairs={{0,2},{2,0},{4,6},{6,4},{8,10},{10,8},{12,14},{14,12},{16,18},{18,... | collective-permute-start | bytes 2660360 | tf_op jit(solution)/shard_map/ppermute | solution.py:592
  90.0 2.7 copy-start.15
  91.8 3.9 copy-start.4
  124.2 15.5 %slice-start = ((s8[4718592]{0:T(1024)(128)(4,1)}), s8[4194304]{0:T(1024)(128)(4,1)S(1)}, s32[]{:S(2)}) async-start(s8[4718592]{0:T(1024)(128)(4,1)} %bitcast.301), calls=%async_computation.1 | async-start | bytes 8388608
  124.3 19.3 %slice-start.4 = ((s8[4718592]{0:T(1024)(128)(4,1)}), s8[4194304]{0:T(1024)(128)(4,1)S(1)}, s32[]{:S(2)}) async-start(s8[4718592]{0:T(1024)(128)(4,1)} %bitcast.305), calls=%async_computation.5 | async-start | bytes 8388608
  124.5 15.2 %copy-start.6 = (bf16[416,768]{1,0:T(8,128)(2,1)}, bf16[416,768]{1,0:T(8,128)(2,1)S(1)}, u32[]{:S(2)}) copy-start(bf16[416,768]{1,0:T(8,128)(2,1)S(1)} %add_convert_fusion.7.n2_ref) | copy-start | bytes 1916932
  124.5 15.2 %copy-start.5 = (bf16[416,768]{1,0:T(8,128)(2,1)S(1)}, bf16[416,768]{1,0:T(8,128)(2,1)}, u32[]{:S(2)}) copy-start(bf16[416,768]{1,0:T(8,128)(2,1)} %get-tuple-element.120.dout_ref) | copy-start | bytes 1916932
  124.6 15.2 %slice-start.1 = ((s8[4718592]{0:T(1024)(128)(4,1)}), s8[524288]{0:T(1024)(128)(4,1)S(1)}, s32[]{:S(2)}) async-start(s8[4718592]{0:T(1024)(128)(4,1)} %bitcast.301), calls=%async_computation.2 | async-start | bytes 1048576
  124.6 19.0 %slice-start.5 = ((s8[4718592]{0:T(1024)(128)(4,1)}), s8[524288]{0:T(1024)(128)(4,1)S(1)}, s32[]{:S(2)}) async-start(s8[4718592]{0:T(1024)(128)(4,1)} %bitcast.305), calls=%async_computation.6 | async-start | bytes 1048576
  143.6 2.6 copy-start.9
  146.2 1.7 copy-start.13
  147.9 1.5 copy-start.7
  149.5 26.0 %copy-start.1 = (f32[416,768]{1,0:T(8,128)S(1)}, f32[416,768]{1,0:T(8,128)}, u32[]{:S(2)}) copy-start(f32[416,768]{1,0:T(8,128)} %get-tuple-element.85) | copy-start | bytes 3833860
  216.4 5.0 %collective-permute-start.18 = (bf16[2,2,2,2,576,128]{5,4,3,2,1,0:T(8,128)(2,1)}, bf16[2,2,2,2,576,128]{5,4,3,2,1,0:T(8,128)(2,1)S(1)}, u32[]{:S(2)}, u32[]{:S(2)}) collective-permute-start(bf16[2,2,2,2,576,128]{5,4,3,2,1,0:T(8,128)(2,1)} %get-tuple-element.58), channel_id=1, source_target_pairs={{0,2},{2,0},{4,6},{6,4},{8,10},{10,8},{12,14},{14,12},{16,18},{18,... | collective-permute-start | bytes 7077896 | tf_op jit(solution)/shard_map/ppermute | solution.py:592
  217.0 7.7 %collective-permute-start.13 = (bf16[2,2,2,2,576,128]{5,4,3,2,1,0:T(8,128)(2,1)}, bf16[2,2,2,2,576,128]{5,4,3,2,1,0:T(8,128)(2,1)S(1)}, u32[]{:S(2)}, u32[]{:S(2)}) collective-permute-start(bf16[2,2,2,2,576,128]{5,4,3,2,1,0:T(8,128)(2,1)} %get-tuple-element.56), channel_id=1, source_target_pairs={{0,2},{2,0},{4,6},{6,4},{8,10},{10,8},{12,14},{14,12},{16,18},{18,... | collective-permute-start | bytes 7077896 | tf_op jit(solution)/shard_map/ppermute | solution.py:592
  217.1 11.1 %collective-permute-start.8 = (bf16[2,2,2,2,592,128]{5,4,3,2,1,0:T(8,128)(2,1)}, bf16[2,2,2,2,592,128]{5,4,3,2,1,0:T(8,128)(2,1)S(1)}, u32[]{:S(2)}, u32[]{:S(2)}) collective-permute-start(bf16[2,2,2,2,592,128]{5,4,3,2,1,0:T(8,128)(2,1)} %get-tuple-element.54), channel_id=1, source_target_pairs={{0,2},{2,0},{4,6},{6,4},{8,10},{10,8},{12,14},{14,12},{16,18},{18,... | collective-permute-start | bytes 7274504 | tf_op jit(solution)/shard_map/ppermute | solution.py:592
  221.4 3.4 copy-start.11
  221.4 9.1 %slice-start.2 = ((s8[4718592]{0:T(1024)(128)(4,1)}), s8[4194304]{0:T(1024)(128)(4,1)S(1)}, s32[]{:S(2)}) async-start(s8[4718592]{0:T(1024)(128)(4,1)} %bitcast.303), calls=%async_computation.3 | async-start | bytes 8388608
  223.8 28.3 %collective-permute-start.19 = (bf16[2,2,2,576,128]{4,3,2,1,0:T(8,128)(2,1)S(1)}, bf16[2,2,2,576,128]{4,3,2,1,0:T(8,128)(2,1)S(1)}, u32[]{:S(2)}, u32[]{:S(2)}) collective-permute-start(bf16[2,2,2,576,128]{4,3,2,1,0:T(8,128)(2,1)S(1)} %get-tuple-element.101), channel_id=1, source_target_pairs={{0,8},{2,10},{4,12},{6,14},{8,0},{10,2},{12,4},{14,6},{16,24},{18,... | collective-permute-start | bytes 3538952 | tf_op jit(solution)/shard_map/ppermute | solution.py:592
  224.8 3.5 copy-start.10
  224.8 5.7 %slice-start.3 = ((s8[4718592]{0:T(1024)(128)(4,1)}), s8[524288]{0:T(1024)(128)(4,1)S(1)}, s32[]{:S(2)}) async-start(s8[4718592]{0:T(1024)(128)(4,1)} %bitcast.303), calls=%async_computation.4 | async-start | bytes 1048576
  225.4 28.6 %collective-permute-start.14 = (bf16[2,2,2,576,128]{4,3,2,1,0:T(8,128)(2,1)S(1)}, bf16[2,2,2,576,128]{4,3,2,1,0:T(8,128)(2,1)S(1)}, u32[]{:S(2)}, u32[]{:S(2)}) collective-permute-start(bf16[2,2,2,576,128]{4,3,2,1,0:T(8,128)(2,1)S(1)} %get-tuple-element.99), channel_id=1, source_target_pairs={{0,4},{2,6},{4,0},{6,2},{8,12},{10,14},{12,8},{14,10},{16,20},{18,... | collective-permute-start | bytes 3538952 | tf_op jit(solution)/shard_map/ppermute | solution.py:592
  228.2 2.2 copy-start.8
  228.9 29.6 %collective-permute-start.9 = (bf16[2,2,2,592,128]{4,3,2,1,0:T(8,128)(2,1)S(1)}, bf16[2,2,2,592,128]{4,3,2,1,0:T(8,128)(2,1)S(1)}, u32[]{:S(2)}, u32[]{:S(2)}) collective-permute-start(bf16[2,2,2,592,128]{4,3,2,1,0:T(8,128)(2,1)S(1)} %get-tuple-element.97), channel_id=1, source_target_pairs={{0,1},{1,0},{2,3},{3,2},{4,5},{5,4},{6,7},{7,6},{8,9},{9,8},{10,11... | collective-permute-start | bytes 3637256 | tf_op jit(solution)/shard_map/ppermute | solution.py:592
  252.4 18.1 %collective-permute-start.20 = (bf16[2,2,576,128]{3,2,1,0:T(8,128)(2,1)S(1)}, bf16[2,2,576,128]{3,2,1,0:T(8,128)(2,1)S(1)}, u32[]{:S(2)}, u32[]{:S(2)}) collective-permute-start(bf16[2,2,576,128]{3,2,1,0:T(8,128)(2,1)S(1)} %get-tuple-element.107), channel_id=1, source_target_pairs={{0,1},{1,0},{2,3},{3,2},{4,5},{5,4},{6,7},{7,6},{8,9},{9,8},{10,11... | collective-permute-start | bytes 1769480 | tf_op jit(solution)/shard_map/ppermute | solution.py:592
  254.3 5.1 %copy-start.2 = (f32[416,768]{1,0:T(8,128)S(1)}, f32[416,768]{1,0:T(8,128)}, u32[]{:S(2)}) copy-start(f32[416,768]{1,0:T(8,128)} %get-tuple-element.83) | copy-start | bytes 3833860
  254.3 5.1 %copy-start.12 = (f32[416,768]{1,0:T(8,128)S(1)}, f32[416,768]{1,0:T(8,128)}, u32[]{:S(2)}) copy-start(f32[416,768]{1,0:T(8,128)} %get-tuple-element.128) | copy-start | bytes 3833860
  254.3 16.9 %collective-permute-start.15 = (bf16[2,2,576,128]{3,2,1,0:T(8,128)(2,1)S(1)}, bf16[2,2,576,128]{3,2,1,0:T(8,128)(2,1)S(1)}, u32[]{:S(2)}, u32[]{:S(2)}) collective-permute-start(bf16[2,2,576,128]{3,2,1,0:T(8,128)(2,1)S(1)} %get-tuple-element.105), channel_id=1, source_target_pairs={{0,8},{2,10},{4,12},{6,14},{8,0},{10,2},{12,4},{14,6},{16,24},{18,... | collective-permute-start | bytes 1769480 | tf_op jit(solution)/shard_map/ppermute | solution.py:592
  258.8 15.1 %collective-permute-start.10 = (bf16[2,2,592,128]{3,2,1,0:T(8,128)(2,1)S(1)}, bf16[2,2,592,128]{3,2,1,0:T(8,128)(2,1)S(1)}, u32[]{:S(2)}, u32[]{:S(2)}) collective-permute-start(bf16[2,2,592,128]{3,2,1,0:T(8,128)(2,1)S(1)} %get-tuple-element.103), channel_id=1, source_target_pairs={{0,4},{2,6},{4,0},{6,2},{8,12},{10,14},{12,8},{14,10},{16,20},{18,... | collective-permute-start | bytes 1818632 | tf_op jit(solution)/shard_map/ppermute | solution.py:592
  270.7 9.0 %collective-permute-start.21 = (bf16[2,576,128]{2,1,0:T(8,128)(2,1)S(1)}, bf16[2,576,128]{2,1,0:T(8,128)(2,1)S(1)}, u32[]{:S(2)}, u32[]{:S(2)}) collective-permute-start(bf16[2,576,128]{2,1,0:T(8,128)(2,1)S(1)} %get-tuple-element.115), channel_id=1, source_target_pairs={{0,4},{2,6},{4,0},{6,2},{8,12},{10,14},{12,8},{14,10},{16,20},{18,... | collective-permute-start | bytes 884744 | tf_op jit(solution)/shard_map/ppermute | solution.py:592
  271.4 11.0 %collective-permute-start.16 = (bf16[2,576,128]{2,1,0:T(8,128)(2,1)S(1)}, bf16[2,576,128]{2,1,0:T(8,128)(2,1)S(1)}, u32[]{:S(2)}, u32[]{:S(2)}) collective-permute-start(bf16[2,576,128]{2,1,0:T(8,128)(2,1)S(1)} %get-tuple-element.113), channel_id=1, source_target_pairs={{0,1},{1,0},{2,3},{3,2},{4,5},{5,4},{6,7},{7,6},{8,9},{9,8},{10,11... | collective-permute-start | bytes 884744 | tf_op jit(solution)/shard_map/ppermute | solution.py:592
  274.1 8.8 %collective-permute-start.11 = (bf16[2,592,128]{2,1,0:T(8,128)(2,1)S(1)}, bf16[2,592,128]{2,1,0:T(8,128)(2,1)S(1)}, u32[]{:S(2)}, u32[]{:S(2)}) collective-permute-start(bf16[2,592,128]{2,1,0:T(8,128)(2,1)S(1)} %get-tuple-element.111), channel_id=1, source_target_pairs={{0,8},{2,10},{4,12},{6,14},{8,0},{10,2},{12,4},{14,6},{16,24},{18,... | collective-permute-start | bytes 909320 | tf_op jit(solution)/shard_map/ppermute | solution.py:592
  279.8 16.3 %collective-permute-start.22 = (bf16[576,128]{1,0:T(8,128)(2,1)S(1)}, bf16[576,128]{1,0:T(8,128)(2,1)S(1)}, u32[]{:S(2)}, u32[]{:S(2)}) collective-permute-start(bf16[576,128]{1,0:T(8,128)(2,1)S(1)} %fusion.72), channel_id=1, source_target_pairs={{0,16},{2,18},{4,20},{6,22},{8,24},{10,26},{12,28},{14,30},{16,0},... | collective-permute-start | bytes 442376 | tf_op jit(solution)/shard_map/ppermute | solution.py:592
  282.4 16.8 %collective-permute-start.17 = (bf16[576,128]{1,0:T(8,128)(2,1)S(1)}, bf16[576,128]{1,0:T(8,128)(2,1)S(1)}, u32[]{:S(2)}, u32[]{:S(2)}) collective-permute-start(bf16[576,128]{1,0:T(8,128)(2,1)S(1)} %fusion.70), channel_id=1, source_target_pairs={{0,16},{2,18},{4,20},{6,22},{8,24},{10,26},{12,28},{14,30},{16,0},... | collective-permute-start | bytes 442376 | tf_op jit(solution)/shard_map/ppermute | solution.py:592
  282.9 18.6 %collective-permute-start.12 = (bf16[592,128]{1,0:T(8,128)(2,1)S(1)}, bf16[592,128]{1,0:T(8,128)(2,1)S(1)}, u32[]{:S(2)}, u32[]{:S(2)}) collective-permute-start(bf16[592,128]{1,0:T(8,128)(2,1)S(1)} %fusion.68), channel_id=1, source_target_pairs={{0,16},{2,18},{4,20},{6,22},{8,24},{10,26},{12,28},{14,30},{16,0},... | collective-permute-start | bytes 454664 | tf_op jit(solution)/shard_map/ppermute | solution.py:592
  377.5 26.6 %collective-permute-start.23 = (bf16[3464,128]{1,0:T(8,128)(2,1)S(1)}, bf16[3464,128]{1,0:T(8,128)(2,1)S(1)}, u32[]{:S(2)}, u32[]{:S(2)}) collective-permute-start(bf16[3464,128]{1,0:T(8,128)(2,1)S(1)} %get-tuple-element.108), channel_id=1, source_target_pairs={{0,1},{1,0},{2,3},{3,2},{4,5},{5,4},{6,7},{7,6},{8,9},{9,8},{10,11... | collective-permute-start | bytes 2660360 | tf_op jit(solution)/shard_map/ppermute | solution.py:592
  404.1 2.6 copy-start.3
  404.1 26.2 %collective-permute-start.24 = (bf16[3464,128]{1,0:T(8,128)(2,1)S(1)}, bf16[3464,128]{1,0:T(8,128)(2,1)}, u32[]{:S(2)}, u32[]{:S(2)}) collective-permute-start(bf16[3464,128]{1,0:T(8,128)(2,1)S(1)} %collective-permute-done.23.refs_5_), channel_id=1, source_target_pairs={{0,4},{2,6},{4,0},{6,2},{8,12},{10,14},{12,8},{14,10},{16,20},{18,... | collective-permute-start | bytes 2660360 | tf_op jit(solution)/shard_map/ppermute | solution.py:592
  404.7 28.0 %collective-permute-start.25 = (bf16[3464,128]{1,0:T(8,128)(2,1)S(1)}, bf16[3464,128]{1,0:T(8,128)(2,1)S(1)}, u32[]{:S(2)}, u32[]{:S(2)}) collective-permute-start(bf16[3464,128]{1,0:T(8,128)(2,1)S(1)} %collective-permute-done.23.refs_5_), channel_id=1, source_target_pairs={{0,8},{2,10},{4,12},{6,14},{8,0},{10,2},{12,4},{14,6},{16,24},{18,... | collective-permute-start | bytes 2660360 | tf_op jit(solution)/shard_map/ppermute | solution.py:592
  406.2 28.9 %collective-permute-start.27 = (bf16[3464,128]{1,0:T(8,128)(2,1)S(1)}, bf16[3464,128]{1,0:T(8,128)(2,1)}, u32[]{:S(2)}, u32[]{:S(2)}) collective-permute-start(bf16[3464,128]{1,0:T(8,128)(2,1)S(1)} %collective-permute-done.23.refs_5_), channel_id=1, source_target_pairs={{0,2},{2,0},{4,6},{6,4},{8,10},{10,8},{12,14},{14,12},{16,18},{18,... | collective-permute-start | bytes 2660360 | tf_op jit(solution)/shard_map/ppermute | solution.py:592
  406.2 27.7 %collective-permute-start.26 = (bf16[3464,128]{1,0:T(8,128)(2,1)S(1)}, bf16[3464,128]{1,0:T(8,128)(2,1)S(1)}, u32[]{:S(2)}, u32[]{:S(2)}) collective-permute-start(bf16[3464,128]{1,0:T(8,128)(2,1)S(1)} %get-tuple-element.73), channel_id=1, source_target_pairs={{0,1},{1,0},{2,3},{3,2},{4,5},{5,4},{6,7},{7,6},{8,9},{9,8},{10,11... | collective-permute-start | bytes 2660360 | tf_op jit(solution)/shard_map/ppermute | solution.py:592
  430.3 7.0 %collective-permute-start.28 = (bf16[3464,128]{1,0:T(8,128)(2,1)}, bf16[3464,128]{1,0:T(8,128)(2,1)S(1)}, u32[]{:S(2)}, u32[]{:S(2)}) collective-permute-start(bf16[3464,128]{1,0:T(8,128)(2,1)} %collective-permute-done.24), channel_id=1, source_target_pairs={{0,2},{2,0},{4,6},{6,4},{8,10},{10,8},{12,14},{14,12},{16,18},{18,... | collective-permute-start | bytes 2660360 | tf_op jit(solution)/shard_map/ppermute | solution.py:592
  432.7 5.6 %collective-permute-start.29 = (bf16[3464,128]{1,0:T(8,128)(2,1)S(1)}, bf16[3464,128]{1,0:T(8,128)(2,1)S(1)}, u32[]{:S(2)}, u32[]{:S(2)}) collective-permute-start(bf16[3464,128]{1,0:T(8,128)(2,1)S(1)} %collective-permute-done.25), channel_id=1, source_target_pairs={{0,2},{2,0},{4,6},{6,4},{8,10},{10,8},{12,14},{14,12},{16,18},{18,... | collective-permute-start | bytes 2660360 | tf_op jit(solution)/shard_map/ppermute | solution.py:592
  433.9 5.3 %collective-permute-start.30 = (bf16[3464,128]{1,0:T(8,128)(2,1)S(1)}, bf16[3464,128]{1,0:T(8,128)(2,1)S(1)}, u32[]{:S(2)}, u32[]{:S(2)}) collective-permute-start(bf16[3464,128]{1,0:T(8,128)(2,1)S(1)} %collective-permute-done.26), channel_id=1, source_target_pairs={{0,2},{2,0},{4,6},{6,4},{8,10},{10,8},{12,14},{14,12},{16,18},{18,... | collective-permute-start | bytes 2660360 | tf_op jit(solution)/shard_map/ppermute | solution.py:592
Sparse Core Ops, SparseCore 0:
  302.6 65.6 all-gather.1
where the time goes:
time: 452 us; the launch traced here: 447 us
  Pallas kernels  172 us (38%)
  waiting for transfers between devices  145 us (32%)
  matrix products  35.9 us (8%)
  local copies, waits for them, and re-layouts  33.5 us (7%)
  starting transfers between devices  27.6 us (6%)
  other arithmetic  18.8 us (4%)
  between operations  14.9 us (3%)
    ppermute x31, waiting for transfers between devices, swap(): lax.ppermute(values, axis, [(i, i ^ bit) for i in range(lax.axis_size(axi...  79.5 us
    all_gather x1, waiting for transfers between devices, body(): totals = lax.all_gather(owned, 'wide', axis=0, tiled=True)  65.2 us
    pallas_call x2, Pallas kernels, adam_rows(): pl.pallas_call(functools.partial(adam_kernel, factor=factor), grid_spec=p...  45.2 us
    pallas_call x1, Pallas kernels, pack_shares(): pl.pallas_call(functools.partial(pack_kernel, part_rows=part_rows, share_...  34.7 us
    ppermute x31, starting transfers between devices, swap(): lax.ppermute(values, axis, [(i, i ^ bit) for i in range(lax.axis_size(axi...  27.6 us
    pallas_call x1, Pallas kernels, attend(): pl.pallas_call(attend_kernel, grid=(wins, pairs), in_specs=[column(0), co...  25.3 us
    pallas_call x1, Pallas kernels, attend_back(): pl.pallas_call(attend_back_kernel, grid=(wins, pairs), in_specs=[column(0...  24.6 us
    pallas_call x1, Pallas kernels, unpack_matrices(): pl.pallas_call(functools.partial(unpack_kernel, plan=plan), grid=(before,...  21.1 us
  transfers between devices with their start and end apart: 32, of which 16 were waited for; matrix products, arithmetic and copies ran while one was open for 8% of the time, Pallas kernels for 13%

commit v1 on v0

--- a/solution.py
+++ b/solution.py
@@ -175,21 +175,19 @@
 def attend_kernel(q_ref, k_ref, v_ref, table_ref, shift_ref, key_ref, probs_ref, out_ref):
     shift = shift_ref[...]
     key_cells = key_ref[...]
-    row_count = shift.shape[0]
-    real_key = lax.broadcasted_iota(jnp.int32, (row_count, row_count), 1) < WS * WS
+    last_lane = lax.broadcasted_iota(jnp.int32, shift.shape, 1) == 127
+    double_cells = jnp.concatenate([key_cells, key_cells], 1)
     for part in range(2):
         cut = slice(part * HD, (part + 1) * HD)
         queries = q_ref[:, cut]
         along = jnp.dot(queries, table_ref[...], preferred_element_type=jnp.float32)
         for bit in (1, 2, 4, 8):
             along = jnp.where((shift & bit) != 0, pltpu.roll(along, 128 - bit, 1), along)
-        high = along.astype(jnp.bfloat16)
-        low = (along - high.astype(jnp.float32)).astype(jnp.bfloat16)
-        scores = dot_last(queries, k_ref[:, cut]) * (1.0 / math.sqrt(HD))
-        scores = scores + dot_last(high, key_cells) + dot_last(low, key_cells)
-        scores = jnp.where(real_key, scores, -1e30)
+        along = jnp.where(last_lane, 1.0, along)
+        scores = dot_last(queries * (1.0 / math.sqrt(HD)), k_ref[:, cut])
+        scores = scores + dot_last(high_low(along), double_cells)
         powers = jnp.exp(scores - jnp.max(scores, -1, keepdims=True))
-        probs = (powers / jnp.sum(powers, -1, keepdims=True)).astype(jnp.bfloat16)
+        probs = (powers * (1.0 / jnp.sum(powers, -1, keepdims=True))).astype(jnp.bfloat16)
         probs_ref[0, part] = probs
         out_ref[:, cut] = jnp.dot(
             probs, v_ref[:, cut], preferred_element_type=jnp.float32
@@ -202,6 +200,7 @@
 ):
     shift = shift_ref[...]
     key_cells = key_ref[...]
+    double_table = jnp.concatenate([table_ref[...], table_ref[...]], 1)
     scale = 1.0 / math.sqrt(HD)
 
     @pl.when((pl.program_id(0) == 0) & (pl.program_id(1) == 0))
@@ -219,15 +218,25 @@
         inner = jnp.sum(wide_probs * grad_probs, -1, keepdims=True)
         grad_scores = (wide_probs * (grad_probs - inner)).astype(jnp.bfloat16)
         dk_ref[:, cut] = (dot_first(grad_scores, queries) * scale).astype(jnp.bfloat16)
-        along = jnp.dot(grad_scores, key_cells, preferred_element_type=jnp.float32)
+        both = jnp.dot(
+            grad_scores,
+            jnp.concatenate([key_cells, k_ref[:, cut]], 1),
+            preferred_element_type=jnp.float32,
+        )
+        along = both[:, :128]
         for bit in (1, 2, 4, 8):
             along = jnp.where((shift & bit) != 0, pltpu.roll(along, bit, 1), along)
-        high = along.astype(jnp.bfloat16)
-        low = (along - high.astype(jnp.float32)).astype(jnp.bfloat16)
-        grad_query = jnp.dot(grad_scores, k_ref[:, cut], preferred_element_type=jnp.float32) * scale
-        grad_query = grad_query + dot_last(high, table_ref[...]) + dot_last(low, table_ref[...])
+        pair = high_low(along)
+        grad_query = both[:, 128:] * scale + dot_last(pair, double_table)
         dq_ref[:, cut] = grad_query.astype(jnp.bfloat16)
-        dtable_ref[...] += dot_first(queries, high) + dot_first(queries, low)
+        table_pair = dot_first(queries, pair)
+        dtable_ref[...] += table_pair[:, :128] + table_pair[:, 128:]
+
+
+def high_low(values):
+    high = values.astype(jnp.bfloat16)
+    low = (values - high.astype(jnp.float32)).astype(jnp.bfloat16)
+    return jnp.concatenate([high, low], 1)
 
 
 def window_constants(row_count):
@@ -239,7 +248,8 @@
     shift = jnp.where(live, shift, 0)
     offset = jnp.where(first, lanes, lanes - 64)
     place = jnp.where(first, cells // WS, cells % WS)
-    key_cells = jnp.where(live & (offset == place), 1.0, 0.0).astype(jnp.bfloat16)
+    key_cells = jnp.where(live & (offset == place), 1.0, 0.0)
+    key_cells = jnp.where((lanes == 127) & ~live, -1e30, key_cells).astype(jnp.bfloat16)
     return shift, key_cells
 
 
@@ -485,9 +495,9 @@
     )(*factors, tail)
 
 
-def gelu_slope(pre_act):
+def gelu_and_slope(pre_act):
     normal_cdf = 0.5 * (1.0 + jax.scipy.special.erf(pre_act / math.sqrt(2.0)))
-    return normal_cdf + pre_act * jnp.exp(-0.5 * pre_act * pre_act) / math.sqrt(2.0 * math.pi)
+    return pre_act * normal_cdf, normal_cdf + pre_act * jnp.exp(-0.5 * pre_act * pre_act) / math.sqrt(2.0 * math.pi)
 
 
 def window_pass(tokens, cotangent, keep_mask, weights):
@@ -536,7 +546,8 @@
     pre_act = jnp.dot(normed_two, fc1_w, preferred_element_type=jnp.float32) + fc1_b.astype(
         jnp.float32
     )
-    activation = jax.nn.gelu(pre_act, approximate=False).astype(jnp.bfloat16)
+    activation, slope = gelu_and_slope(pre_act)
+    activation = activation.astype(jnp.bfloat16)
     result = keep_rows * (
         resid
         + jnp.dot(activation, fc2_w, preferred_element_type=jnp.float32)
@@ -545,7 +556,7 @@
     cot_rows = cotangent.reshape(row_count, feature).astype(jnp.float32) * keep_rows
     grad_out = cot_rows.astype(jnp.bfloat16)
     grad_act = jnp.einsum("nd,fd->nf", grad_out, fc2_w, preferred_element_type=jnp.float32)
-    grad_pre = (grad_act * gelu_slope(pre_act)).astype(jnp.bfloat16)
+    grad_pre = (grad_act * slope).astype(jnp.bfloat16)
     grad_norm_two = jnp.einsum("nf,df->nd", grad_pre, fc1_w, preferred_element_type=jnp.float32)
     grad_ln2_g = jnp.sum(grad_norm_two * hat_two, 0)
     grad_ln2_b = jnp.sum(grad_norm_two, 0)

time: 452 us -> 437 us (0.967)
  matrix products: 35.9 us -> 26.4 us
    dot_general x1, matrix products: 15.1 us -> 5.82 us  [window_pass(): jnp.dot(normed_two, fc1_w, preferred_element_type=jnp.float32)]
where the time goes in v1:
time: 437 us; the launch traced here: 436 us
  Pallas kernels  170 us (39%)
  waiting for transfers between devices  145 us (33%)
  local copies, waits for them, and re-layouts  33.5 us (8%)
  starting transfers between devices  27.8 us (6%)
  matrix products  26.4 us (6%)
  other arithmetic  18.8 us (4%)
  between operations  14.6 us (3%)
    ppermute x31, waiting for transfers between devices, swap(): lax.ppermute(values, axis, [(i, i ^ bit) for i in range(lax.axis_size(axi...  79.6 us
    all_gather x1, waiting for transfers between devices, body(): totals = lax.all_gather(owned, 'wide', axis=0, tiled=True)  65.3 us
    pallas_call x2, Pallas kernels, adam_rows(): pl.pallas_call(functools.partial(adam_kernel, factor=factor), grid_spec=p...  45.2 us
    pallas_call x1, Pallas kernels, pack_shares(): pl.pallas_call(functools.partial(pack_kernel, part_rows=part_rows, share_...  34.6 us
    ppermute x31, starting transfers between devices, swap(): lax.ppermute(values, axis, [(i, i ^ bit) for i in range(lax.axis_size(axi...  27.7 us
    pallas_call x1, Pallas kernels, attend(): pl.pallas_call(attend_kernel, grid=(wins, pairs), in_specs=[column(0), co...  25.3 us
    pallas_call x1, Pallas kernels, attend_back(): pl.pallas_call(attend_back_kernel, grid=(wins, pairs), in_specs=[column(0...  23.1 us
    pallas_call x1, Pallas kernels, unpack_matrices(): pl.pallas_call(functools.partial(unpack_kernel, plan=plan), grid=(before,...  21.1 us
  transfers between devices with their start and end apart: 32, of which 16 were waited for; matrix products, arithmetic and copies ran while one was open for 8% of the time, Pallas kernels for 13%

profile of v1, /device:TPU:0, one launch (start us, length us, event | category | flops | bytes accessed | tf_op | source)
XLA Modules:
  0.0 435.7 jit_solution(1769552958238705731)
XLA Ops:
  7.3 3.5 fusion.35
  10.8 3.0 collective-permute-start
  14.6 1.2 multiply_reduce_fusion.5
  16.6 12.8 %place_own.1 = bf16[2,27712,128]{2,1,0:T(8,128)(2,1)} custom-call(s32[1]{0:T(128)} %bitcast.2.group_ref, f32[27712,128]{1,0:T(8,128)} %master_ref.7), custom_call_target="tpu_custom_call" | custom-call | tf_op jit(solution)/shard_map/place_own/pallas_call | solution.py:694
  32.3 1.4 collective-permute-done
  33.8 1.7 collective-permute-start.1
  35.5 1.6 collective-permute-start.2
  37.0 1.5 collective-permute-start.3
  38.6 2.1 bitcast_dynamic-update-slice_fusion.15
  40.7 14.1 %collective-permute-done.1 = bf16[3464,128]{1,0:T(8,128)(2,1)S(1)} collective-permute-done((bf16[3464,128]{1,0:T(8,128)(2,1)}, bf16[3464,128]{1,0:T(8,128)(2,1)S(1)}, u32[]{:S(2)}, u32[]{:S(2)}) %collective-permute-start.1) | collective-permute-done | bytes 886816 | tf_op jit(solution)/shard_map/ppermute | solution.py:603
  54.8 1.2 collective-permute-done.2
  56.0 3.4 collective-permute-done.3
  59.4 1.0 bitcast_dynamic-update-slice_fusion.14
  60.3 1.0 bitcast_dynamic-update-slice_fusion.13
  61.3 1.0 bitcast_dynamic-update-slice_fusion.12
  62.3 1.0 bitcast_dynamic-update-slice_fusion.11
  63.3 1.0 bitcast_dynamic-update-slice_fusion.10
  64.2 1.0 bitcast_dynamic-update-slice_fusion.9
  65.2 1.0 bitcast_dynamic-update-slice_fusion.8
  67.0 21.1 %unpack_matrices.1 = (bf16[768,2304]{1,0:T(8,128)(2,1)}, bf16[768,768]{1,0:T(8,128)(2,1)}, bf16[768,3072]{1,0:T(8,128)(2,1)}, bf16[3072,768]{1,0:T(8,128)(2,1)}) custom-call(bf16[55424,128]{1,0:T(8,128)(2,1)} %bitcast.284), custom_call_target="tpu_custom_call" | custom-call | tf_op jit(solution)/shard_map/unpack_matrices/pallas_call | solution.py:111
  90.0 1.7 multiply_convert_fusion.1
  92.7 3.0 fusion.6.q_ref.k_ref.v_ref
  96.4 25.3 %attend.1 = (bf16[2,12,208,208]{3,2,1,0:T(8,128)(2,1)}, bf16[416,768]{1,0:T(8,128)(2,1)}) custom-call(bf16[416,2304]{1,0:T(8,128)(2,1)} %fusion.6.q_ref.k_ref.v_ref, bf16[416,2304]{1,0:T(8,128)(2,1)} %fusion.6.q_ref.k_ref.v_ref, bf16[416,2304]{1,0:T(8,128)(2,1)} %fusion.6.q_ref.k_ref.v_ref, bf16[64,128]{1,0:T(8,128)(2,1)} %pad_maximum_fusion.1.table_ref, ...), custom_call_target="tpu_custom_call" | custom-call | tf_op jit(solution)/shard_map/attend/pallas_call | solution.py:266
  121.7 2.3 fusion.84
  124.6 5.8 %multiply_convert_fusion = (bf16[416,3072]{1,0:T(8,128)(2,1)}, f32[416,3072]{1,0:T(8,128)S(1)}) fusion(f32[3072]{0:T(1024)S(1)} %fusion.64, bf16[416,768]{1,0:T(8,128)(2,1)S(1)} %add_convert_fusion.7.n2_ref, bf16[768,3072]{1,0:T(8,128)(2,1)} %get-tuple-element.48), kind=kOutput, calls=%fused_computation.7 | convolution fusion | flops 1970601984 | bytes 13037568 | tf_op jit(solution)/shard_map/dot_general | solution.py:546
  130.4 3.6 fusion.5.dpre_ref
  134.1 2.6 multiply_reduce_fusion.1
  136.7 1.7 fusion.80
  138.4 1.5 convolution_convert_fusion.grad_ref
  139.9 23.1 %attend_back.1 = (bf16[416,768]{1,0:T(8,128)(2,1)}, bf16[416,768]{1,0:T(8,128)(2,1)}, bf16[416,768]{1,0:T(8,128)(2,1)}, f32[64,128]{1,0:T(8,128)}) custom-call(bf16[416,2304]{1,0:T(8,128)(2,1)} %fusion.6.q_ref.k_ref.v_ref, bf16[416,2304]{1,0:T(8,128)(2,1)} %fusion.6.q_ref.k_ref.v_ref, bf16[416,2304]{1,0:T(8,128)(2,1)} %fusion.6.q_ref.k_ref.v_ref, ...), custom_call_target="tpu_custom_call" | custom-call | tf_op jit(solution)/shard_map/attend_back/pallas_call | solution.py:288
  164.4 5.5 %multiply_reduce_fusion = (f32[416]{0:T(512)S(1)}, f32[768]{0:T(1024)S(1)}, f32[416]{0:T(512)S(1)}, f32[768]{0:T(1024)S(1)}, f32[416,768]{1,0:T(8,128)}) fusion(f32[416,768]{1,0:T(8,128)S(1)} %copy-done.1, f32[768]{0:T(1024)S(1)} %get-tuple-element.93, bf16[768,2304]{1,0:T(8,128)(2,1)} %get-tuple-element.43, bf16[416,768]{1,0:T(8,128)(2,1)} %get-tuple-element.51.dv_ref, ...), kind=kOutput, calls=%fused_computation.41 | convolution fusion | flops 1480505088 | bytes 8025984 | tf_op jit(solution)/shard_map/nf,df->nd/dot_general | solution.py:576
  170.6 34.6 %pack_grads.1 = (bf16[2,2,2,2,592,128]{5,4,3,2,1,0:T(8,128)(2,1)}, bf16[2,2,2,2,576,128]{5,4,3,2,1,0:T(8,128)(2,1)}, bf16[2,2,2,2,576,128]{5,4,3,2,1,0:T(8,128)(...) custom-call(bf16[416,768]{1,0:T(8,128)(2,1)} %copy-done.4, ...), custom_call_target="tpu_custom_call" | custom-call | tf_op jit(solution)/shard_map/pack_grads/pallas_call | solution.py:474
  206.2 3.9 collective-permute-done.18
  210.0 2.4 add_convert_fusion.3
  214.6 2.2 collective-permute-done.8
  217.5 1.6 collective-permute-start.9
  219.1 2.1 fusion.20
  221.3 19.5 %collective-permute-done.19 = bf16[2,2,2,576,128]{4,3,2,1,0:T(8,128)(2,1)S(1)} collective-permute-done((bf16[2,2,2,576,128]{4,3,2,1,0:T(8,128)(2,1)S(1)}, bf16[2,2,2,576,128]{4,3,2,1,0:T(8,128)(2,1)S(1)}, u32[]{:S(2)}, u32[]{:S(2)}) %collective-permute-start.19) | collective-permute-done | bytes 1179680 | tf_op jit(solution)/shard_map/ppermute | solution.py:603
  241.0 1.6 collective-permute-start.20
  243.6 3.5 collective-permute-done.9
  248.5 1.3 copy.65
  249.8 1.3 copy.64
  251.1 8.1 %collective-permute-done.20 = bf16[2,2,576,128]{3,2,1,0:T(8,128)(2,1)S(1)} collective-permute-done((bf16[2,2,576,128]{3,2,1,0:T(8,128)(2,1)S(1)}, bf16[2,2,576,128]{3,2,1,0:T(8,128)(2,1)S(1)}, u32[]{:S(2)}, u32[]{:S(2)}) %collective-permute-start.20) | collective-permute-done | bytes 589856 | tf_op jit(solution)/shard_map/ppermute | solution.py:603
  260.1 1.6 collective-permute-start.16
  263.2 5.1 %collective-permute-done.21 = bf16[2,576,128]{2,1,0:T(8,128)(2,1)S(1)} collective-permute-done((bf16[2,576,128]{2,1,0:T(8,128)(2,1)S(1)}, bf16[2,576,128]{2,1,0:T(8,128)(2,1)S(1)}, u32[]{:S(2)}, u32[]{:S(2)}) %collective-permute-start.21) | collective-permute-done | bytes 294944 | tf_op jit(solution)/shard_map/ppermute | solution.py:603
  268.4 2.7 collective-permute-start.22
  271.5 2.7 collective-permute-start.12
  274.2 10.5 %collective-permute-done.22 = bf16[576,128]{1,0:T(8,128)(2,1)S(1)} collective-permute-done((bf16[576,128]{1,0:T(8,128)(2,1)S(1)}, bf16[576,128]{1,0:T(8,128)(2,1)S(1)}, u32[]{:S(2)}, u32[]{:S(2)}) %collective-permute-start.22) | collective-permute-done | bytes 147488 | tf_op jit(solution)/shard_map/ppermute | solution.py:603
  284.7 3.1 collective-permute-done.17
  287.9 2.3 collective-permute-done.12
  291.7 65.3 %all-gather.2.cloned.1.call-done.total_ref = bf16[27904,128]{1,0:T(8,128)(2,1)} async-done(((bf16[1744,128]{1,0:T(8,128)(2,1)}), bf16[27904,128]{1,0:T(8,128)(2,1)}) %all-gather.2.cloned.1.call-update) | async-done | bytes 7143440 | tf_op jit(solution)/shard_map/all_gather | solution.py:796
  356.9 7.7 %eighth_weights.1 = bf16[2,3464,128]{2,1,0:T(8,128)(2,1)} custom-call(s32[2]{0:T(128)} %pad_add_fusion.spot_ref, bf16[27904,128]{1,0:T(8,128)(2,1)} %all-gather.2.cloned.1.call-done.total_ref, f32[27712,128]{1,0:T(8,128)} %master_ref.7, f32[27712,128]{1,0:T(8,128)} %first_ref.5, f32[27712,128]{1,0:T(8,128)} %second_ref.5), custom_call_target="tpu_custom_call" | custom-call | tf_op jit(solution)/shard_map/eighth_weights/pallas_call | solution.py:717
  364.6 1.5 slice_bitcast_fusion
  366.2 1.5 collective-permute-start.23
  367.7 23.8 %adam_rows.2 = (f32[27712,128]{1,0:T(8,128)}, f32[27712,128]{1,0:T(8,128)}, f32[27712,128]{1,0:T(8,128)}, f32[27712,128]{1,0:T(8,128)}, bf16[2,27712,128]{2,1,0:T(8,128)(2,1)}) custom-call(s32[1]{0:T(128)} %bitcast.2.group_ref, bf16[27904,128]{1,0:T(8,128)(2,1)} %all-gather.2.cloned.1.call-done.total_ref, ...), custom_call_target="tpu_custom_call", output_to_operand_aliasing={{4}: (5, {})} | custom-call | tf_op jit(solution)/shard_map/adam_rows/pallas_call | solution.py:749
  391.5 1.3 multiply_bitcast_fusion
  393.3 1.5 collective-permute-start.25
  395.4 21.4 %adam_rows.3 = (f32[27712,128]{1,0:T(8,128)}, f32[27712,128]{1,0:T(8,128)}, f32[27712,128]{1,0:T(8,128)}, f32[27712,128]{1,0:T(8,128)}, bf16[2,27712,128]{2,1,0:T(8,128)(2,1)}) custom-call(s32[1]{0:T(128)} %bitcast.2.group_ref, ...), custom_call_target="tpu_custom_call", output_to_operand_aliasing={{0}: (5, {}), {1}: (6, {}), {2}: (7, {}), {3}: (8, {}), {4}... | custom-call | tf_op jit(solution)/shard_map/adam_rows/pallas_call | solution.py:749
  416.9 2.1 bitcast_dynamic-update-slice_fusion.7
  419.2 2.1 bitcast_dynamic-update-slice_fusion.6
  423.8 2.1 bitcast_dynamic-update-slice_fusion.3
  426.0 1.0 bitcast_dynamic-update-slice_fusion.2
  426.9 1.0 bitcast_dynamic-update-slice_fusion.1
  427.9 1.0 bitcast_dynamic-update-slice_fusion
  (164 shorter events, 26.3 us)
Async XLA Ops:
  7.2 6.6 %copy-start.16 = (s32[2,1]{0,1:T(1,128)S(1)}, s32[2,1]{0,1:T(1,128)}, u32[]{:S(2)}) copy-start(s32[2,1]{0,1:T(1,128)} %param.8) | copy-start | bytes 28
  7.2 6.7 %copy-start = (bf16[2,1,196,768]{3,0,2,1:T(2,128)(2,1)S(1)}, bf16[2,1,196,768]{3,0,2,1:T(2,128)(2,1)}, u32[]{:S(2)}) copy-start(bf16[2,1,196,768]{3,0,2,1:T(2,128)(2,1)} %param.6) | copy-start | bytes 1806340
  7.2 349.7 %all-gather.2.cloned.1.call-start = ((), (), s32[]{:S(2)}) async-start(), calls=%async_computation | async-start | bytes 7589888 | tf_op jit(solution)/shard_map/all_gather | solution.py:796
  10.8 23.0 %collective-permute-start = (bf16[3464,128]{1,0:T(8,128)(2,1)}, bf16[3464,128]{1,0:T(8,128)(2,1)}, u32[]{:S(2)}, u32[]{:S(2)}) collective-permute-start(bf16[3464,128]{1,0:T(8,128)(2,1)} %get-tuple-element.94), channel_id=1, source_target_pairs={{0,1},{1,0},{2,3},{3,2},{4,5},{5,4},{6,7},{7,6},{8,9},{9,8},{10,11... | collective-permute-start | bytes 2660360 | tf_op jit(solution)/shard_map/ppermute | solution.py:603
  29.4 1.1 copy-start.14
  33.8 21.1 %collective-permute-start.1 = (bf16[3464,128]{1,0:T(8,128)(2,1)}, bf16[3464,128]{1,0:T(8,128)(2,1)S(1)}, u32[]{:S(2)}, u32[]{:S(2)}) collective-permute-start(bf16[3464,128]{1,0:T(8,128)(2,1)} %collective-permute-done), channel_id=1, source_target_pairs={{0,4},{2,6},{4,0},{6,2},{8,12},{10,14},{12,8},{14,10},{16,20},{18,... | collective-permute-start | bytes 2660360 | tf_op jit(solution)/shard_map/ppermute | solution.py:603
  35.5 20.5 %collective-permute-start.2 = (bf16[3464,128]{1,0:T(8,128)(2,1)}, bf16[3464,128]{1,0:T(8,128)(2,1)S(1)}, u32[]{:S(2)}, u32[]{:S(2)}) collective-permute-start(bf16[3464,128]{1,0:T(8,128)(2,1)} %collective-permute-done), channel_id=1, source_target_pairs={{0,8},{2,10},{4,12},{6,14},{8,0},{10,2},{12,4},{14,6},{16,24},{18,... | collective-permute-start | bytes 2660360 | tf_op jit(solution)/shard_map/ppermute | solution.py:603
  37.0 25.2 %collective-permute-start.4 = (bf16[3464,128]{1,0:T(8,128)(2,1)}, bf16[3464,128]{1,0:T(8,128)(2,1)S(1)}, u32[]{:S(2)}, u32[]{:S(2)}) collective-permute-start(bf16[3464,128]{1,0:T(8,128)(2,1)} %collective-permute-done), channel_id=1, source_target_pairs={{0,2},{2,0},{4,6},{6,4},{8,10},{10,8},{12,14},{14,12},{16,18},{18,... | collective-permute-start | bytes 2660360 | tf_op jit(solution)/shard_map/ppermute | solution.py:603
  37.0 22.3 %collective-permute-start.3 = (bf16[3464,128]{1,0:T(8,128)(2,1)}, bf16[3464,128]{1,0:T(8,128)(2,1)S(1)}, u32[]{:S(2)}, u32[]{:S(2)}) collective-permute-start(bf16[3464,128]{1,0:T(8,128)(2,1)} %get-tuple-element.42), channel_id=1, source_target_pairs={{0,1},{1,0},{2,3},{3,2},{4,5},{5,4},{6,7},{7,6},{8,9},{9,8},{10,11... | collective-permute-start | bytes 2660360 | tf_op jit(solution)/shard_map/ppermute | solution.py:603
  54.8 8.4 %collective-permute-start.5 = (bf16[3464,128]{1,0:T(8,128)(2,1)S(1)}, bf16[3464,128]{1,0:T(8,128)(2,1)S(1)}, u32[]{:S(2)}, u32[]{:S(2)}) collective-permute-start(bf16[3464,128]{1,0:T(8,128)(2,1)S(1)} %collective-permute-done.1), channel_id=1, source_target_pairs={{0,2},{2,0},{4,6},{6,4},{8,10},{10,8},{12,14},{14,12},{16,18},{18,... | collective-permute-start | bytes 2660360 | tf_op jit(solution)/shard_map/ppermute | solution.py:603
  56.0 8.3 %collective-permute-start.6 = (bf16[3464,128]{1,0:T(8,128)(2,1)S(1)}, bf16[3464,128]{1,0:T(8,128)(2,1)S(1)}, u32[]{:S(2)}, u32[]{:S(2)}) collective-permute-start(bf16[3464,128]{1,0:T(8,128)(2,1)S(1)} %collective-permute-done.2), channel_id=1, source_target_pairs={{0,2},{2,0},{4,6},{6,4},{8,10},{10,8},{12,14},{14,12},{16,18},{18,... | collective-permute-start | bytes 2660360 | tf_op jit(solution)/shard_map/ppermute | solution.py:603
  59.4 5.8 %collective-permute-start.7 = (bf16[3464,128]{1,0:T(8,128)(2,1)S(1)}, bf16[3464,128]{1,0:T(8,128)(2,1)S(1)}, u32[]{:S(2)}, u32[]{:S(2)}) collective-permute-start(bf16[3464,128]{1,0:T(8,128)(2,1)S(1)} %collective-permute-done.3), channel_id=1, source_target_pairs={{0,2},{2,0},{4,6},{6,4},{8,10},{10,8},{12,14},{14,12},{16,18},{18,... | collective-permute-start | bytes 2660360 | tf_op jit(solution)/shard_map/ppermute | solution.py:603
  90.0 2.7 copy-start.15
  91.8 3.9 copy-start.4
  124.2 6.2 %slice-start = ((s8[4718592]{0:T(1024)(128)(4,1)}), s8[4194304]{0:T(1024)(128)(4,1)S(1)}, s32[]{:S(2)}) async-start(s8[4718592]{0:T(1024)(128)(4,1)} %bitcast.301), calls=%async_computation.1 | async-start | bytes 8388608
  124.5 5.9 %copy-start.6 = (bf16[416,768]{1,0:T(8,128)(2,1)}, bf16[416,768]{1,0:T(8,128)(2,1)S(1)}, u32[]{:S(2)}) copy-start(bf16[416,768]{1,0:T(8,128)(2,1)S(1)} %add_convert_fusion.7.n2_ref) | copy-start | bytes 1916932
  124.5 5.9 %copy-start.5 = (bf16[416,768]{1,0:T(8,128)(2,1)S(1)}, bf16[416,768]{1,0:T(8,128)(2,1)}, u32[]{:S(2)}) copy-start(bf16[416,768]{1,0:T(8,128)(2,1)} %get-tuple-element.120.dout_ref) | copy-start | bytes 1916932
  124.5 5.9 %slice-start.1 = ((s8[4718592]{0:T(1024)(128)(4,1)}), s8[524288]{0:T(1024)(128)(4,1)S(1)}, s32[]{:S(2)}) async-start(s8[4718592]{0:T(1024)(128)(4,1)} %bitcast.301), calls=%async_computation.2 | async-start | bytes 1048576
  124.5 9.5 %slice-start.4 = ((s8[4718592]{0:T(1024)(128)(4,1)}), s8[4194304]{0:T(1024)(128)(4,1)S(1)}, s32[]{:S(2)}) async-start(s8[4718592]{0:T(1024)(128)(4,1)} %bitcast.305), calls=%async_computation.5 | async-start | bytes 8388608
  130.4 3.7 slice-start.5
  134.1 2.6 copy-start.9
  136.7 1.7 copy-start.13
  138.4 1.5 copy-start.7
  139.9 24.4 %copy-start.1 = (f32[416,768]{1,0:T(8,128)S(1)}, f32[416,768]{1,0:T(8,128)}, u32[]{:S(2)}) copy-start(f32[416,768]{1,0:T(8,128)} %get-tuple-element.85) | copy-start | bytes 3833860
  205.1 4.9 %collective-permute-start.18 = (bf16[2,2,2,2,576,128]{5,4,3,2,1,0:T(8,128)(2,1)}, bf16[2,2,2,2,576,128]{5,4,3,2,1,0:T(8,128)(2,1)S(1)}, u32[]{:S(2)}, u32[]{:S(2)}) collective-permute-start(bf16[2,2,2,2,576,128]{5,4,3,2,1,0:T(8,128)(2,1)} %get-tuple-element.58), channel_id=1, source_target_pairs={{0,2},{2,0},{4,6},{6,4},{8,10},{10,8},{12,14},{14,12},{16,18},{18,... | collective-permute-start | bytes 7077896 | tf_op jit(solution)/shard_map/ppermute | solution.py:603
  205.6 7.7 %collective-permute-start.13 = (bf16[2,2,2,2,576,128]{5,4,3,2,1,0:T(8,128)(2,1)}, bf16[2,2,2,2,576,128]{5,4,3,2,1,0:T(8,128)(2,1)S(1)}, u32[]{:S(2)}, u32[]{:S(2)}) collective-permute-start(bf16[2,2,2,2,576,128]{5,4,3,2,1,0:T(8,128)(2,1)} %get-tuple-element.56), channel_id=1, source_target_pairs={{0,2},{2,0},{4,6},{6,4},{8,10},{10,8},{12,14},{14,12},{16,18},{18,... | collective-permute-start | bytes 7077896 | tf_op jit(solution)/shard_map/ppermute | solution.py:603
  205.7 11.1 %collective-permute-start.8 = (bf16[2,2,2,2,592,128]{5,4,3,2,1,0:T(8,128)(2,1)}, bf16[2,2,2,2,592,128]{5,4,3,2,1,0:T(8,128)(2,1)S(1)}, u32[]{:S(2)}, u32[]{:S(2)}) collective-permute-start(bf16[2,2,2,2,592,128]{5,4,3,2,1,0:T(8,128)(2,1)} %get-tuple-element.54), channel_id=1, source_target_pairs={{0,2},{2,0},{4,6},{6,4},{8,10},{10,8},{12,14},{14,12},{16,18},{18,... | collective-permute-start | bytes 7274504 | tf_op jit(solution)/shard_map/ppermute | solution.py:603
  210.0 3.4 copy-start.11
  210.0 9.1 %slice-start.2 = ((s8[4718592]{0:T(1024)(128)(4,1)}), s8[4194304]{0:T(1024)(128)(4,1)S(1)}, s32[]{:S(2)}) async-start(s8[4718592]{0:T(1024)(128)(4,1)} %bitcast.303), calls=%async_computation.3 | async-start | bytes 8388608
  212.4 28.3 %collective-permute-start.19 = (bf16[2,2,2,576,128]{4,3,2,1,0:T(8,128)(2,1)S(1)}, bf16[2,2,2,576,128]{4,3,2,1,0:T(8,128)(2,1)S(1)}, u32[]{:S(2)}, u32[]{:S(2)}) collective-permute-start(bf16[2,2,2,576,128]{4,3,2,1,0:T(8,128)(2,1)S(1)} %get-tuple-element.101), channel_id=1, source_target_pairs={{0,8},{2,10},{4,12},{6,14},{8,0},{10,2},{12,4},{14,6},{16,24},{18,... | collective-permute-start | bytes 3538952 | tf_op jit(solution)/shard_map/ppermute | solution.py:603
  213.4 3.5 copy-start.10
  213.4 5.7 %slice-start.3 = ((s8[4718592]{0:T(1024)(128)(4,1)}), s8[524288]{0:T(1024)(128)(4,1)S(1)}, s32[]{:S(2)}) async-start(s8[4718592]{0:T(1024)(128)(4,1)} %bitcast.303), calls=%async_computation.4 | async-start | bytes 1048576
  214.0 28.6 %collective-permute-start.14 = (bf16[2,2,2,576,128]{4,3,2,1,0:T(8,128)(2,1)S(1)}, bf16[2,2,2,576,128]{4,3,2,1,0:T(8,128)(2,1)S(1)}, u32[]{:S(2)}, u32[]{:S(2)}) collective-permute-start(bf16[2,2,2,576,128]{4,3,2,1,0:T(8,128)(2,1)S(1)} %get-tuple-element.99), channel_id=1, source_target_pairs={{0,4},{2,6},{4,0},{6,2},{8,12},{10,14},{12,8},{14,10},{16,20},{18,... | collective-permute-start | bytes 3538952 | tf_op jit(solution)/shard_map/ppermute | solution.py:603
  216.9 2.2 copy-start.8
  217.5 29.6 %collective-permute-start.9 = (bf16[2,2,2,592,128]{4,3,2,1,0:T(8,128)(2,1)S(1)}, bf16[2,2,2,592,128]{4,3,2,1,0:T(8,128)(2,1)S(1)}, u32[]{:S(2)}, u32[]{:S(2)}) collective-permute-start(bf16[2,2,2,592,128]{4,3,2,1,0:T(8,128)(2,1)S(1)} %get-tuple-element.97), channel_id=1, source_target_pairs={{0,1},{1,0},{2,3},{3,2},{4,5},{5,4},{6,7},{7,6},{8,9},{9,8},{10,11... | collective-permute-start | bytes 3637256 | tf_op jit(solution)/shard_map/ppermute | solution.py:603
  241.0 18.1 %collective-permute-start.20 = (bf16[2,2,576,128]{3,2,1,0:T(8,128)(2,1)S(1)}, bf16[2,2,576,128]{3,2,1,0:T(8,128)(2,1)S(1)}, u32[]{:S(2)}, u32[]{:S(2)}) collective-permute-start(bf16[2,2,576,128]{3,2,1,0:T(8,128)(2,1)S(1)} %get-tuple-element.107), channel_id=1, source_target_pairs={{0,1},{1,0},{2,3},{3,2},{4,5},{5,4},{6,7},{7,6},{8,9},{9,8},{10,11... | collective-permute-start | bytes 1769480 | tf_op jit(solution)/shard_map/ppermute | solution.py:603
  243.0 5.1 %copy-start.2 = (f32[416,768]{1,0:T(8,128)S(1)}, f32[416,768]{1,0:T(8,128)}, u32[]{:S(2)}) copy-start(f32[416,768]{1,0:T(8,128)} %get-tuple-element.83) | copy-start | bytes 3833860
  243.0 5.1 %copy-start.12 = (f32[416,768]{1,0:T(8,128)S(1)}, f32[416,768]{1,0:T(8,128)}, u32[]{:S(2)}) copy-start(f32[416,768]{1,0:T(8,128)} %get-tuple-element.128) | copy-start | bytes 3833860
  243.0 16.9 %collective-permute-start.15 = (bf16[2,2,576,128]{3,2,1,0:T(8,128)(2,1)S(1)}, bf16[2,2,576,128]{3,2,1,0:T(8,128)(2,1)S(1)}, u32[]{:S(2)}, u32[]{:S(2)}) collective-permute-start(bf16[2,2,576,128]{3,2,1,0:T(8,128)(2,1)S(1)} %get-tuple-element.105), channel_id=1, source_target_pairs={{0,8},{2,10},{4,12},{6,14},{8,0},{10,2},{12,4},{14,6},{16,24},{18,... | collective-permute-start | bytes 1769480 | tf_op jit(solution)/shard_map/ppermute | solution.py:603
  247.4 15.1 %collective-permute-start.10 = (bf16[2,2,592,128]{3,2,1,0:T(8,128)(2,1)S(1)}, bf16[2,2,592,128]{3,2,1,0:T(8,128)(2,1)S(1)}, u32[]{:S(2)}, u32[]{:S(2)}) collective-permute-start(bf16[2,2,592,128]{3,2,1,0:T(8,128)(2,1)S(1)} %get-tuple-element.103), channel_id=1, source_target_pairs={{0,4},{2,6},{4,0},{6,2},{8,12},{10,14},{12,8},{14,10},{16,20},{18,... | collective-permute-start | bytes 1818632 | tf_op jit(solution)/shard_map/ppermute | solution.py:603
  259.3 9.0 %collective-permute-start.21 = (bf16[2,576,128]{2,1,0:T(8,128)(2,1)S(1)}, bf16[2,576,128]{2,1,0:T(8,128)(2,1)S(1)}, u32[]{:S(2)}, u32[]{:S(2)}) collective-permute-start(bf16[2,576,128]{2,1,0:T(8,128)(2,1)S(1)} %get-tuple-element.115), channel_id=1, source_target_pairs={{0,4},{2,6},{4,0},{6,2},{8,12},{10,14},{12,8},{14,10},{16,20},{18,... | collective-permute-start | bytes 884744 | tf_op jit(solution)/shard_map/ppermute | solution.py:603
  260.1 11.0 %collective-permute-start.16 = (bf16[2,576,128]{2,1,0:T(8,128)(2,1)S(1)}, bf16[2,576,128]{2,1,0:T(8,128)(2,1)S(1)}, u32[]{:S(2)}, u32[]{:S(2)}) collective-permute-start(bf16[2,576,128]{2,1,0:T(8,128)(2,1)S(1)} %get-tuple-element.113), channel_id=1, source_target_pairs={{0,1},{1,0},{2,3},{3,2},{4,5},{5,4},{6,7},{7,6},{8,9},{9,8},{10,11... | collective-permute-start | bytes 884744 | tf_op jit(solution)/shard_map/ppermute | solution.py:603
  262.7 8.8 %collective-permute-start.11 = (bf16[2,592,128]{2,1,0:T(8,128)(2,1)S(1)}, bf16[2,592,128]{2,1,0:T(8,128)(2,1)S(1)}, u32[]{:S(2)}, u32[]{:S(2)}) collective-permute-start(bf16[2,592,128]{2,1,0:T(8,128)(2,1)S(1)} %get-tuple-element.111), channel_id=1, source_target_pairs={{0,8},{2,10},{4,12},{6,14},{8,0},{10,2},{12,4},{14,6},{16,24},{18,... | collective-permute-start | bytes 909320 | tf_op jit(solution)/shard_map/ppermute | solution.py:603
  268.4 16.3 %collective-permute-start.22 = (bf16[576,128]{1,0:T(8,128)(2,1)S(1)}, bf16[576,128]{1,0:T(8,128)(2,1)S(1)}, u32[]{:S(2)}, u32[]{:S(2)}) collective-permute-start(bf16[576,128]{1,0:T(8,128)(2,1)S(1)} %fusion.62), channel_id=1, source_target_pairs={{0,16},{2,18},{4,20},{6,22},{8,24},{10,26},{12,28},{14,30},{16,0},... | collective-permute-start | bytes 442376 | tf_op jit(solution)/shard_map/ppermute | solution.py:603
  271.1 16.8 %collective-permute-start.17 = (bf16[576,128]{1,0:T(8,128)(2,1)S(1)}, bf16[576,128]{1,0:T(8,128)(2,1)S(1)}, u32[]{:S(2)}, u32[]{:S(2)}) collective-permute-start(bf16[576,128]{1,0:T(8,128)(2,1)S(1)} %fusion.60), channel_id=1, source_target_pairs={{0,16},{2,18},{4,20},{6,22},{8,24},{10,26},{12,28},{14,30},{16,0},... | collective-permute-start | bytes 442376 | tf_op jit(solution)/shard_map/ppermute | solution.py:603
  271.5 18.7 %collective-permute-start.12 = (bf16[592,128]{1,0:T(8,128)(2,1)S(1)}, bf16[592,128]{1,0:T(8,128)(2,1)S(1)}, u32[]{:S(2)}, u32[]{:S(2)}) collective-permute-start(bf16[592,128]{1,0:T(8,128)(2,1)S(1)} %fusion.58), channel_id=1, source_target_pairs={{0,16},{2,18},{4,20},{6,22},{8,24},{10,26},{12,28},{14,30},{16,0},... | collective-permute-start | bytes 454664 | tf_op jit(solution)/shard_map/ppermute | solution.py:603
  366.2 26.6 %collective-permute-start.23 = (bf16[3464,128]{1,0:T(8,128)(2,1)S(1)}, bf16[3464,128]{1,0:T(8,128)(2,1)S(1)}, u32[]{:S(2)}, u32[]{:S(2)}) collective-permute-start(bf16[3464,128]{1,0:T(8,128)(2,1)S(1)} %get-tuple-element.108), channel_id=1, source_target_pairs={{0,1},{1,0},{2,3},{3,2},{4,5},{5,4},{6,7},{7,6},{8,9},{9,8},{10,11... | collective-permute-start | bytes 2660360 | tf_op jit(solution)/shard_map/ppermute | solution.py:603
  392.8 2.6 copy-start.3
  392.8 26.2 %collective-permute-start.24 = (bf16[3464,128]{1,0:T(8,128)(2,1)S(1)}, bf16[3464,128]{1,0:T(8,128)(2,1)}, u32[]{:S(2)}, u32[]{:S(2)}) collective-permute-start(bf16[3464,128]{1,0:T(8,128)(2,1)S(1)} %collective-permute-done.23.refs_5_), channel_id=1, source_target_pairs={{0,4},{2,6},{4,0},{6,2},{8,12},{10,14},{12,8},{14,10},{16,20},{18,... | collective-permute-start | bytes 2660360 | tf_op jit(solution)/shard_map/ppermute | solution.py:603
  393.3 28.0 %collective-permute-start.25 = (bf16[3464,128]{1,0:T(8,128)(2,1)S(1)}, bf16[3464,128]{1,0:T(8,128)(2,1)S(1)}, u32[]{:S(2)}, u32[]{:S(2)}) collective-permute-start(bf16[3464,128]{1,0:T(8,128)(2,1)S(1)} %collective-permute-done.23.refs_5_), channel_id=1, source_target_pairs={{0,8},{2,10},{4,12},{6,14},{8,0},{10,2},{12,4},{14,6},{16,24},{18,... | collective-permute-start | bytes 2660360 | tf_op jit(solution)/shard_map/ppermute | solution.py:603
  394.9 28.9 %collective-permute-start.27 = (bf16[3464,128]{1,0:T(8,128)(2,1)S(1)}, bf16[3464,128]{1,0:T(8,128)(2,1)}, u32[]{:S(2)}, u32[]{:S(2)}) collective-permute-start(bf16[3464,128]{1,0:T(8,128)(2,1)S(1)} %collective-permute-done.23.refs_5_), channel_id=1, source_target_pairs={{0,2},{2,0},{4,6},{6,4},{8,10},{10,8},{12,14},{14,12},{16,18},{18,... | collective-permute-start | bytes 2660360 | tf_op jit(solution)/shard_map/ppermute | solution.py:603
  394.9 27.7 %collective-permute-start.26 = (bf16[3464,128]{1,0:T(8,128)(2,1)S(1)}, bf16[3464,128]{1,0:T(8,128)(2,1)S(1)}, u32[]{:S(2)}, u32[]{:S(2)}) collective-permute-start(bf16[3464,128]{1,0:T(8,128)(2,1)S(1)} %get-tuple-element.73), channel_id=1, source_target_pairs={{0,1},{1,0},{2,3},{3,2},{4,5},{5,4},{6,7},{7,6},{8,9},{9,8},{10,11... | collective-permute-start | bytes 2660360 | tf_op jit(solution)/shard_map/ppermute | solution.py:603
  419.0 7.0 %collective-permute-start.28 = (bf16[3464,128]{1,0:T(8,128)(2,1)}, bf16[3464,128]{1,0:T(8,128)(2,1)S(1)}, u32[]{:S(2)}, u32[]{:S(2)}) collective-permute-start(bf16[3464,128]{1,0:T(8,128)(2,1)} %collective-permute-done.24), channel_id=1, source_target_pairs={{0,2},{2,0},{4,6},{6,4},{8,10},{10,8},{12,14},{14,12},{16,18},{18,... | collective-permute-start | bytes 2660360 | tf_op jit(solution)/shard_map/ppermute | solution.py:603
  421.4 5.6 %collective-permute-start.29 = (bf16[3464,128]{1,0:T(8,128)(2,1)S(1)}, bf16[3464,128]{1,0:T(8,128)(2,1)S(1)}, u32[]{:S(2)}, u32[]{:S(2)}) collective-permute-start(bf16[3464,128]{1,0:T(8,128)(2,1)S(1)} %collective-permute-done.25), channel_id=1, source_target_pairs={{0,2},{2,0},{4,6},{6,4},{8,10},{10,8},{12,14},{14,12},{16,18},{18,... | collective-permute-start | bytes 2660360 | tf_op jit(solution)/shard_map/ppermute | solution.py:603
  422.6 5.3 %collective-permute-start.30 = (bf16[3464,128]{1,0:T(8,128)(2,1)S(1)}, bf16[3464,128]{1,0:T(8,128)(2,1)S(1)}, u32[]{:S(2)}, u32[]{:S(2)}) collective-permute-start(bf16[3464,128]{1,0:T(8,128)(2,1)S(1)} %collective-permute-done.26), channel_id=1, source_target_pairs={{0,2},{2,0},{4,6},{6,4},{8,10},{10,8},{12,14},{14,12},{16,18},{18,... | collective-permute-start | bytes 2660360 | tf_op jit(solution)/shard_map/ppermute | solution.py:603
Sparse Core Ops, SparseCore 0:
  291.2 65.6 all-gather.1
